TPU v7x, 32 devices: a whole 2x2x4 slice. The times are simulated.
32 devices in a mesh: layer: 4 (over z), tile: 8 (over y, x, core).
Axes of the slice: x: 2, y: 2, z: 4, core: 2. Of those that a mesh axis runs over, the one named last changes fastest.
Arguments:
- measured_slopes: float32 [6, 2, 96, 4096], P(None, None, 'tile'), may hold values from -18 to 18
- valid_mask: int32 [96, 4096], P('tile'), may hold values 0 or 1
- layer_offsets: int32 [6, 4, 2], replicated, may hold values from -8 to 8, as said below
- reg_weight: float32 [4], replicated, may hold values from 0.01 to 0.1
Outputs:
- layer_estimate: float32 [4, 96, 4096], P('layer', 'tile')
- residual: float32 [4, 96, 4096], P('layer', 'tile')
Inputs may be any that keep to these rules, and one draw needn't show every extreme that they name: `layer_offsets`: every entry lies between -8 and 8; some entry equals 8 and some equals -8.
All inputs are finite; a program needn't handle non-finite values. No bound on the sum of `valid_mask` on one device may be relied on, other than what follows from the above.
Results may differ from a plain program's by a relative error of at most 0.0001.
Values sent between devices are 32-bit elements; how exact they have to be, the bound alone decides.
No kernel may reach another device: no remote copies, remote signals or barrier semaphores. Data moves between devices by JAX's collectives and lax.ppermute only.
A program may use at most 64 MiB of HBM per device.

v0:
```python
import jax
import jax.numpy as jnp
from jax import lax
from jax.sharding import PartitionSpec as P

LAY_DEV = 1
HALO = 8
ITERS = 2


def shifted(value, axis, steps):
    count = lax.axis_size(axis)
    first, last = (max(0, -steps), min(count, count - steps))
    return lax.ppermute(value, axis, [(source, source + steps) for source in range(first, last)])


def padded_2(cells, sides, width):
    for axis, dim in sides:
        count = lax.axis_size(axis)
        ends = count - 1
        head = lax.slice_in_dim(cells, 0, width, axis=dim)
        tail = lax.slice_in_dim(cells, cells.shape[dim] - width, cells.shape[dim], axis=dim)
        cells = jnp.concatenate(
            [
                lax.ppermute(tail, axis, [(i, (i + 1) % count) for i in range(ends)]),
                cells,
                lax.ppermute(head, axis, [((i + 1) % count, i) for i in range(ends)]),
            ],
            axis=dim,
        )
    return cells


def laplace_rows(field):
    padded = jnp.pad(field, ((0, 0), (0, 0), (1, 1)))
    center = field[:, 1:-1]
    return 4.0 * center - field[:, :-2] - field[:, 2:] - padded[:, 1:-1, :-2] - padded[:, 1:-1, 2:]


def per_device(measured_slopes, valid_mask, layer_offsets, reg_weight):
    rows = measured_slopes.shape[2]
    width = measured_slopes.shape[3]
    total_rows = rows * lax.axis_size("tile")
    first_row = lax.axis_index("tile") * rows
    layer_first = lax.axis_index("layer") * LAY_DEV
    maskf = valid_mask.astype(jnp.float32)
    own_offsets = lax.dynamic_slice_in_dim(layer_offsets, layer_first, LAY_DEV, 1)
    own_reg = lax.dynamic_slice_in_dim(reg_weight, layer_first, LAY_DEV, 0)

    def inside(start, count):
        index = first_row + start + jnp.arange(count)
        return ((index >= 0) & (index < total_rows)).astype(jnp.float32)[:, None]

    def left_of(field):
        return jnp.pad(field, ((0, 0), (0, 0), (1, 0)))[..., :width]

    def adjoint_field(slope_x, slope_y):
        above_x, above_y = shifted((slope_x[:, rows - 1 :], slope_y[:, rows - 1 :]), "tile", 1)
        upper_x = jnp.concatenate([above_x, slope_x[:, : rows - 1]], 1)
        summed_x = slope_x + upper_x
        summed_y = slope_y + left_of(slope_y)
        summed_above = above_y + left_of(above_y)
        upper_y = jnp.concatenate([summed_above, summed_y[:, : rows - 1]], 1)
        adjoint = 0.5 * (left_of(summed_x) - summed_x + upper_y - summed_y)
        return padded_2(adjoint, (("tile", 1),), HALO)

    def back_project(adjoint_ext):
        padded = jnp.pad(adjoint_ext, ((0, 0), (0, 0), (HALO, HALO)))

        def back_window(field, offset):
            return lax.dynamic_slice(field, (HALO - offset[0], HALO - offset[1]), (rows, width))

        result = [jnp.sum(jax.vmap(back_window)(padded, own_offsets[:, 0]), axis=0)]
        return jnp.stack(result)

    def squares(field):
        return lax.psum(jnp.sum(field * field), ("layer", "tile"))

    right_side = back_project(
        adjoint_field(maskf * measured_slopes[:, 0], maskf * measured_slopes[:, 1])
    )
    estimate = jnp.zeros_like(right_side)
    residual = right_side
    direction = right_side
    norm_now = squares(residual)
    for step in range(ITERS):
        apply_extended = padded_2(direction, (("tile", 1),), HALO + 1)
        project_padded = jnp.pad(apply_extended, ((0, 0), (0, 0), (HALO, HALO)))
        layer_pad = project_padded[0]

        def project_window(offset):
            return lax.dynamic_slice(
                layer_pad, (HALO + 1 + offset[0], HALO + offset[1]), (rows + 1, width)
            )

        total = jax.vmap(project_window)(own_offsets[:, 0])
        apply_phase = lax.psum(total, "layer")
        apply_phase = apply_phase * inside(0, rows + 1)[None]
        slopes_padded = jnp.pad(apply_phase, ((0, 0), (0, 0), (0, 1)))
        p00 = slopes_padded[:, :rows, :width]
        p01 = slopes_padded[:, :rows, 1:]
        p10 = slopes_padded[:, 1:, :width]
        p11 = slopes_padded[:, 1:, 1:]
        grad_x = 0.5 * (p01 - p00 + p11 - p10)
        grad_y = 0.5 * (p10 - p00 + p11 - p01)
        apply_slope_x = maskf * grad_x
        apply_slope_y = maskf * grad_y
        projected = back_project(adjoint_field(apply_slope_x, apply_slope_y))
        smoothed = (
            laplace_rows(apply_extended[:, HALO - 1 : HALO + rows + 3]) * inside(-1, rows + 2)[None]
        )
        image = projected + own_reg[:, None, None] * laplace_rows(smoothed)
        alpha = norm_now / lax.psum(jnp.sum(direction * image), ("layer", "tile"))
        estimate = estimate + alpha * direction
        residual = residual - alpha * image
        if step + 1 < ITERS:
            norm_next = squares(residual)
            direction = residual + norm_next / norm_now * direction
            norm_now = norm_next
    return (estimate, residual)


def solution(mesh):
    return jax.shard_map(
        per_device,
        mesh=mesh,
        in_specs=(P(None, None, "tile", None), P("tile", None), P(), P()),
        out_specs=(P("layer", "tile", None), P("layer", "tile", None)),
        check_vma=False,
    )
```

profile of v0, /device:TPU:0, one launch (start us, length us, event | category | flops | bytes accessed | tf_op | source)
XLA Modules:
  0.0 525.0 jit_solution(12211578822455936179)
XLA Ops:
  7.2 4.9 fusion.36
  18.9 5.2 collective-permute-start.1
  28.8 6.5 %collective-permute-start.2 = (f32[6,8,4096]{2,1,0:T(8,128)}, f32[6,8,4096]{2,1,0:T(8,128)}, u32[]{:S(2)}, u32[]{:S(2)}) collective-permute-start(f32[6,8,4096]{2,1,0:T(8,128)} %get-tuple-element.111), channel_id=1, source_target_pairs={{0,1},{1,2},{2,3},{3,4},{4,5},{5,6},{6,7},{8,9},{9,10},{10,11},{11... | collective-permute-start | bytes 2359304 | tf_op jit(solution)/shard_map/ppermute | solution.py:25
  36.6 3.9 select_maximum_fusion.4
  40.7 22.2 %while.5 = (s32[]{:T(128)}, f32[6,28,4112]{2,1,0:T(8,128)}, s32[6,3]{0,1:T(4,128)S(1)}, f32[6,12,4096]{2,1,0:T(8,128)S(1)}, s32[]{:T(128)}) while((s32[]{:T(128)}, f32[6,28,4112]{2,1,0:T(8,128)}, s32[6,3]{0,1:T(4,128)S(1)}, f32[6,12,4096]{2,1,0:T(8,128)S(1)}, s32[]{:T(128)}) %tuple.97), condition=%wide.while_cond, body=%wide.while_body.sunk | while | flops 2 | bytes 458889 | solution.py:71
  63.3 13.8 %collective-permute-start.4 = (f32[1,9,4096]{2,0,1:T(1,128)S(1)}, f32[1,9,4096]{2,0,1:T(1,128)S(1)}, u32[]{:S(2)}, u32[]{:S(2)}) collective-permute-start(f32[1,9,4096]{2,0,1:T(1,128)S(1)} %get-tuple-element.119), channel_id=1, source_target_pairs={{0,1},{1,2},{2,3},{3,4},{4,5},{5,6},{6,7},{8,9},{9,10},{10,11},{11... | collective-permute-start | bytes 442376 | tf_op jit(solution)/shard_map/ppermute | solution.py:25
  81.1 13.1 %while.6 = (s32[]{:T(128)}, f32[30,4112]{1,0:T(8,128)S(1)}, s32[6,2]{0,1:T(2,128)S(1)}, f32[6,13,4096]{2,1,0:T(8,128)S(1)}, s32[]{:T(128)}) while((s32[]{:T(128)}, f32[30,4112]{1,0:T(8,128)S(1)}, s32[6,2]{0,1:T(2,128)S(1)}, f32[6,13,4096]{2,1,0:T(8,128)S(1)}, s32[]{:T(128)}) %tuple.100), condition=%wide.while_cond.1, body=%wide.while_body.1.sunk | while | flops 2 | bytes 524405 | solution.py:92
  97.0 78.0 %all-reduce.24.cloned.1.call-done = f32[6,13,4096]{2,1,0:T(8,128)} async-done(((f32[6,13,4096]{2,1,0:T(8,128)}), f32[6,13,4096]{2,1,0:T(8,128)}) %all-reduce.24.cloned.1.call-update) | async-done | bytes 1277968 | tf_op jit(solution)/shard_map/psum | solution.py:97
  180.3 4.1 collective-permute-start.6
  188.0 3.3 collective-permute-start.8
  195.6 20.6 %while.7 = (s32[]{:T(128)}, f32[6,28,4112]{2,1,0:T(8,128)S(1)}, s32[6,3]{0,1:T(4,128)S(1)}, f32[6,12,4096]{2,1,0:T(8,128)}, s32[]{:T(128)}) while((s32[]{:T(128)}, f32[6,28,4112]{2,1,0:T(8,128)S(1)}, s32[6,3]{0,1:T(4,128)S(1)}, f32[6,12,4096]{2,1,0:T(8,128)}, s32[]{:T(128)}) %tuple.116), condition=%wide.while_cond.2, body=%wide.while_body.2.sunk | while | flops 2 | bytes 460413 | solution.py:71
  219.7 56.5 %all-reduce.20 = (f32[]{:T(128)}, f32[]{:T(128)}) all-reduce(f32[]{:T(128)} %multiply_reduce_fusion, f32[]{:T(128)} %get-tuple-element.86), channel_id=1, replica_groups=mesh['layer'=4,'tile'=8] {'layer','tile'}, use_global_device_ids=true, to_apply=%region_2.3 | all-reduce | flops 2 | bytes 16 | tf_op jit(solution)/shard_map/psum | solution.py:77
  278.6 40.0 %psum.45 = f32[]{:T(128)} all-reduce(f32[]{:T(128)} %multiply_reduce_fusion.2), channel_id=1, replica_groups=mesh['layer'=4,'tile'=8] {'layer','tile'}, use_global_device_ids=true, to_apply=%region_8.9 | all-reduce | flops 1 | bytes 8 | tf_op jit(solution)/shard_map/psum | solution.py:77
  321.6 3.3 collective-permute-start.10
  327.0 12.7 %while.8 = (s32[]{:T(128)}, f32[30,4112]{1,0:T(8,128)S(1)}, s32[6,2]{0,1:T(2,128)S(1)}, f32[6,13,4096]{2,1,0:T(8,128)S(1)}, s32[]{:T(128)}) while((s32[]{:T(128)}, f32[30,4112]{1,0:T(8,128)S(1)}, s32[6,2]{0,1:T(2,128)S(1)}, f32[6,13,4096]{2,1,0:T(8,128)S(1)}, s32[]{:T(128)}) %tuple.118), condition=%wide.while_cond.3, body=%wide.while_body.3.sunk | while | flops 2 | bytes 524405 | solution.py:92
  340.9 72.5 %all-reduce.26.cloned.1.call-done = f32[6,13,4096]{2,1,0:T(8,128)} async-done(((f32[6,13,4096]{2,1,0:T(8,128)}), f32[6,13,4096]{2,1,0:T(8,128)}) %all-reduce.26.cloned.1.call-update) | async-done | bytes 1277968 | tf_op jit(solution)/shard_map/psum | solution.py:97
  418.7 4.1 collective-permute-start.12
  426.6 3.3 collective-permute-start.14
  434.6 22.3 %while.9 = (s32[]{:T(128)}, f32[6,28,4112]{2,1,0:T(8,128)}, s32[6,3]{0,1:T(4,128)S(1)}, f32[6,12,4096]{2,1,0:T(8,128)S(1)}, s32[]{:T(128)}) while((s32[]{:T(128)}, f32[6,28,4112]{2,1,0:T(8,128)}, s32[6,3]{0,1:T(4,128)S(1)}, f32[6,12,4096]{2,1,0:T(8,128)S(1)}, s32[]{:T(128)}) %tuple.117), condition=%wide.while_cond.4, body=%wide.while_body.4.sunk | while | flops 2 | bytes 458889 | solution.py:71
  435.3 3.0 dynamic-slice_dynamic-update-slice_fusion.8
  439.0 3.0 dynamic-slice_dynamic-update-slice_fusion.8
  442.7 3.0 dynamic-slice_dynamic-update-slice_fusion.8
  446.4 3.0 dynamic-slice_dynamic-update-slice_fusion.8
  459.1 56.5 %psum.47 = f32[]{:T(128)} all-reduce(f32[]{:T(128)} %get-tuple-element.84), channel_id=1, replica_groups=mesh['layer'=4,'tile'=8] {'layer','tile'}, use_global_device_ids=true, to_apply=%region_12.13 | all-reduce | flops 1 | bytes 8 | tf_op jit(solution)/shard_map/psum | solution.py:113
  (212 shorter events, 137.5 us)
Async XLA Ops:
  7.2 28.1 %copy-start = (s32[6,4,2]{0,2,1:T(2,128)S(1)}, s32[6,4,2]{0,2,1:T(2,128)}, u32[]{:S(2)}) copy-start(s32[6,4,2]{0,2,1:T(2,128)} %param.6) | copy-start | bytes 580
  7.2 167.8 %all-reduce.24.cloned.1.call-start = ((), (), s32[]{:S(2)}) async-start(), calls=%async_computation | async-start | bytes 3145728 | tf_op jit(solution)/shard_map/psum | solution.py:97
  13.1 3.3 collective-permute-start
  18.9 6.1 %collective-permute-start.1 = (f32[6,1,4096]{2,1,0:T(1,128)S(1)}, f32[6,1,4096]{2,1,0:T(1,128)S(1)}, u32[]{:S(2)}, u32[]{:S(2)}) collective-permute-start(f32[6,1,4096]{2,1,0:T(1,128)S(1)} %slice.348), channel_id=1, source_target_pairs={{0,1},{1,2},{2,3},{3,4},{4,5},{5,6},{6,7},{8,9},{9,10},{10,11},{11... | collective-permute-start | bytes 294920 | tf_op jit(solution)/shard_map/ppermute | solution.py:14
  27.5 7.9 %collective-permute-start.3 = (f32[6,8,4096]{2,1,0:T(8,128)}, f32[6,8,4096]{2,1,0:T(8,128)S(1)}, u32[]{:S(2)}, u32[]{:S(2)}) collective-permute-start(f32[6,8,4096]{2,1,0:T(8,128)} %get-tuple-element.112), channel_id=1, source_target_pairs={{1,0},{2,1},{3,2},{4,3},{5,4},{6,5},{7,6},{9,8},{10,9},{11,10},{12... | collective-permute-start | bytes 2359304 | tf_op jit(solution)/shard_map/ppermute | solution.py:27
  28.8 7.9 %collective-permute-start.2 = (f32[6,8,4096]{2,1,0:T(8,128)}, f32[6,8,4096]{2,1,0:T(8,128)}, u32[]{:S(2)}, u32[]{:S(2)}) collective-permute-start(f32[6,8,4096]{2,1,0:T(8,128)} %get-tuple-element.111), channel_id=1, source_target_pairs={{0,1},{1,2},{2,3},{3,4},{4,5},{5,6},{6,7},{8,9},{9,10},{10,11},{11... | collective-permute-start | bytes 2359304 | tf_op jit(solution)/shard_map/ppermute | solution.py:25
  63.3 15.1 %collective-permute-start.4 = (f32[1,9,4096]{2,0,1:T(1,128)S(1)}, f32[1,9,4096]{2,0,1:T(1,128)S(1)}, u32[]{:S(2)}, u32[]{:S(2)}) collective-permute-start(f32[1,9,4096]{2,0,1:T(1,128)S(1)} %get-tuple-element.119), channel_id=1, source_target_pairs={{0,1},{1,2},{2,3},{3,4},{4,5},{5,6},{6,7},{8,9},{9,10},{10,11},{11... | collective-permute-start | bytes 442376 | tf_op jit(solution)/shard_map/ppermute | solution.py:25
  77.2 3.3 collective-permute-start.5
  81.1 14.5 %copy-start.14 = (f32[4]{0:T(128)S(1)}, f32[4]{0:T(128)}, u32[]{:S(2)}) copy-start(f32[4]{0:T(128)} %param.7) | copy-start | bytes 52
  95.4 318.0 %all-reduce.26.cloned.1.call-start = ((), (), s32[]{:S(2)}) async-start(), calls=%async_computation.1 | async-start | bytes 3145728 | tf_op jit(solution)/shard_map/psum | solution.py:97
  96.3 80.3 %copy-start.7 = (f32[12,4096]{1,0:T(8,128)}, f32[12,4096]{1,0:T(8,128)S(1)}, u32[]{:S(2)}) copy-start(f32[12,4096]{1,0:T(8,128)S(1)} %broadcast_multiply_fusion.2) | copy-start | bytes 589828
  178.4 6.0 %collective-permute-start.7 = (f32[6,1,4096]{2,1,0:T(1,128)S(1)}, f32[6,1,4096]{2,1,0:T(1,128)S(1)}, u32[]{:S(2)}, u32[]{:S(2)}) collective-permute-start(f32[6,1,4096]{2,1,0:T(1,128)S(1)} %slice.358), channel_id=1, source_target_pairs={{0,1},{1,2},{2,3},{3,4},{4,5},{5,6},{6,7},{8,9},{9,10},{10,11},{11... | collective-permute-start | bytes 294920 | tf_op jit(solution)/shard_map/ppermute | solution.py:14
  180.3 5.0 collective-permute-start.6
  186.7 6.3 %collective-permute-start.9 = (f32[6,8,4096]{2,1,0:T(8,128)S(1)}, f32[6,8,4096]{2,1,0:T(8,128)S(1)}, u32[]{:S(2)}, u32[]{:S(2)}) collective-permute-start(f32[6,8,4096]{2,1,0:T(8,128)S(1)} %get-tuple-element.110), channel_id=1, source_target_pairs={{1,0},{2,1},{3,2},{4,3},{5,4},{6,5},{7,6},{9,8},{10,9},{11,10},{12... | collective-permute-start | bytes 2359304 | tf_op jit(solution)/shard_map/ppermute | solution.py:27
  188.0 5.1 collective-permute-start.8
  320.3 4.6 collective-permute-start.11
  321.6 4.0 collective-permute-start.10
  326.3 14.5 %copy-start.5 = (f32[1,30,4096]{2,0,1:T(1,128)}, f32[1,30,4096]{2,0,1:T(1,128)S(1)}, u32[]{:S(2)}) copy-start(f32[1,30,4096]{2,0,1:T(1,128)S(1)} %pad_maximum_fusion) | copy-start | bytes 1474564
  340.9 74.2 %copy-start.8 = (f32[12,4096]{1,0:T(8,128)S(1)}, f32[12,4096]{1,0:T(8,128)}, u32[]{:S(2)}) copy-start(f32[12,4096]{1,0:T(8,128)} %copy-done.7) | copy-start | bytes 589828
  416.8 6.0 %collective-permute-start.13 = (f32[6,1,4096]{2,1,0:T(1,128)S(1)}, f32[6,1,4096]{2,1,0:T(1,128)S(1)}, u32[]{:S(2)}, u32[]{:S(2)}) collective-permute-start(f32[6,1,4096]{2,1,0:T(1,128)S(1)} %slice.373), channel_id=1, source_target_pairs={{0,1},{1,2},{2,3},{3,4},{4,5},{5,6},{6,7},{8,9},{9,10},{10,11},{11... | collective-permute-start | bytes 294920 | tf_op jit(solution)/shard_map/ppermute | solution.py:14
  418.7 5.0 collective-permute-start.12
  425.1 5.9 %collective-permute-start.15 = (f32[6,8,4096]{2,1,0:T(8,128)S(1)}, f32[6,8,4096]{2,1,0:T(8,128)S(1)}, u32[]{:S(2)}, u32[]{:S(2)}) collective-permute-start(f32[6,8,4096]{2,1,0:T(8,128)S(1)} %get-tuple-element.108), channel_id=1, source_target_pairs={{1,0},{2,1},{3,2},{4,3},{5,4},{6,5},{7,6},{9,8},{10,9},{11,10},{12... | collective-permute-start | bytes 2359304 | tf_op jit(solution)/shard_map/ppermute | solution.py:27
  426.6 5.1 collective-permute-start.14
  456.9 61.2 %copy-start.1 = (s32[6,4,2]{0,2,1:T(2,128)S(1)}, s32[6,4,2]{0,2,1:T(2,128)}, u32[]{:S(2)}) copy-start(s32[6,4,2]{0,2,1:T(2,128)} %param.6) | copy-start | bytes 580
  (10 other events, 29.6 us)
Sparse Core Ops, SparseCore 0:
  95.5 79.4 all-reduce.23
  341.0 72.3 all-reduce.25
where the time goes:
time: 527 us; the launch traced here: 525 us
  waiting for transfers between devices  158 us (30%)
  blocking collectives  153 us (29%)
  local copies, waits for them, and re-layouts  104 us (20%)
  starting transfers between devices  55.4 us (11%)
  other arithmetic  35.5 us (7%)
  between operations  18.8 us (4%)
    psum x2, waiting for transfers between devices, per_device(): apply_phase = lax.psum(total, 'layer')  151 us
    psum x2, blocking collectives, squares(): return lax.psum(jnp.sum(field * field), ('layer', 'tile'))  96.5 us
    gather x90, local copies, waits for them, and re-layouts  90.2 us
    psum x1, blocking collectives, per_device(): alpha = norm_now / lax.psum(jnp.sum(direction * image), ('layer', 'tile'))  56.5 us
    ppermute x5, starting transfers between devices, padded_2(): lax.ppermute(tail, axis, [(i, (i + 1) % count) for i in range(ends)])  30.2 us
    ppermute x6, starting transfers between devices, shifted(): lax.ppermute(value, axis, [(source, source + steps) for source in range(f...  18.4 us
  transfers between devices with their start and end apart: 18, of which 11 were waited for; matrix products, arithmetic and copies ran while one was open for 1% of the time, Pallas kernels for 0%

commit v1 on v0

v1 whole, which is shorter than its diff:
```python
import functools

import jax
import jax.numpy as jnp
from jax import lax
from jax.experimental import pallas as pl
from jax.experimental.pallas import tpu as pltpu
from jax.sharding import PartitionSpec as P

HALO = 8
LANES = 128
PAD = 8
REACH_ROW = 2 * (2 * HALO + 1)
REACH = REACH_ROW + HALO + 1
VMEM = pltpu.MemorySpace.VMEM
SMEM = pltpu.MemorySpace.SMEM


def round_up(value, unit):
    return -(-value // unit) * unit


class Plan:
    def __init__(self, mesh, dirs, rows, width, layers):
        self.layer_devices = mesh.shape["layer"]
        self.tiles = mesh.shape["tile"]
        self.devices = self.layer_devices * self.tiles
        self.dirs = dirs
        self.rows = rows
        self.width = width
        self.layers = layers
        self.own_layers = layers // self.layer_devices
        self.grid_rows = rows * self.tiles
        assert width % self.devices == 0 and layers % self.layer_devices == 0
        self.own = width // self.devices
        self.part = width // self.layer_devices
        assert self.part % LANES == 0
        self.lane_tiles = round_up(self.own + 2 * REACH, LANES) // LANES
        self.side = (self.lane_tiles * LANES - self.own) // 2
        self.margin = round_up(self.side + 1, LANES)
        self.strip = self.part + 2 * self.margin
        self.in_rows = round_up(dirs * (rows + 1) + rows, 8)
        self.out_rows = round_up(3 * self.own_layers * rows + 1, 8)


def lane_index():
    return lax.broadcasted_iota(jnp.int32, (8, LANES), 1)


def tall(mask, rows):
    return jnp.broadcast_to(mask[:1], (rows, LANES))


def lane_shift(tiles, steps, rows):
    count = len(tiles)
    if isinstance(steps, int):
        turn = (-steps) % LANES
    else:
        turn = jnp.where(steps > 0, LANES - steps, -steps)
    turned = [pltpu.roll(tile, turn, 1) for tile in tiles]
    if count == 1:
        return turned
    source = lane_index() + steps
    past = tall(source >= LANES, rows)
    before = tall(source < 0, rows)
    if count == 2:
        outside = past | before
        return [jnp.where(outside, turned[1 - t], turned[t]) for t in range(2)]
    return [
        jnp.where(
            past,
            turned[(t + 1) % count],
            jnp.where(before, turned[(t - 1) % count], turned[t]),
        )
        for t in range(count)
    ]


def gather_kernel(plan, place, slopes, mask, out, raw, raw_mask, tall_a, tall_b, strip, sems):
    layer = place[0]
    margin, part = plan.margin, plan.part
    rows, dirs = plan.rows, plan.dirs
    last = plan.layer_devices - 1
    start = pl.multiple_of(layer * part, LANES)

    def copies(source, size, target):
        return (
            pltpu.make_async_copy(
                slopes.at[:, :, :, pl.ds(source, size)],
                raw.at[:, :, :, pl.ds(target, size)],
                sems.at[0],
            ),
            pltpu.make_async_copy(
                mask.at[:, pl.ds(source, size)], raw_mask.at[:, pl.ds(target, size)], sems.at[1]
            ),
        )

    def blank(target):
        raw[:, :, :, target : target + margin] = jnp.zeros((dirs, 2, rows, margin), jnp.float32)
        raw_mask[:, target : target + margin] = jnp.zeros((rows, margin), jnp.int32)

    middle = copies(start, part, margin)
    for copy in middle:
        copy.start()
    for copy in middle:
        copy.wait()

    @pl.when(layer > 0)
    def _():
        left = copies(pl.multiple_of(start - margin, LANES), margin, 0)
        for copy in left:
            copy.start()
        for copy in left:
            copy.wait()

    @pl.when(layer == 0)
    def _():
        blank(0)

    @pl.when(layer < last)
    def _():
        right = copies(pl.multiple_of(start + part, LANES), margin, margin + part)
        for copy in right:
            copy.start()
        for copy in right:
            copy.wait()

    @pl.when(layer == last)
    def _():
        blank(margin + part)

    keep = raw_mask[...].astype(jnp.float32)
    zero_tail = jnp.zeros((16 * (-(-(rows + 1) // 16)) - rows, plan.strip), jnp.float32)
    tall_a[rows:, :] = zero_tail
    tall_b[rows:, :] = zero_tail
    column = lax.broadcasted_iota(jnp.int32, (1, plan.strip), 1) + (start - margin)
    in_grid = jnp.where((column >= 0) & (column < plan.width), 1.0, 0.0)
    strips = plan.strip // LANES
    for n in range(strips):
        lanes = slice(n * LANES, (n + 1) * LANES)
        strip[n, dirs * rows : (dirs + 1) * rows, :] = keep[:, lanes]
        used = dirs * (rows + 1) + rows
        if used < plan.in_rows:
            strip[n, used:, :] = jnp.zeros((plan.in_rows - used, LANES), jnp.float32)
    for g in range(dirs):
        slope_x = raw[g, 0]
        slope_y = raw[g, 1]
        tall_a[:rows, :] = keep * (slope_x + slope_y)
        tall_b[:rows, :] = keep * (slope_x - slope_y)
        both, diff = tall_a[...], tall_b[...]
        shifted_c = pltpu.roll(diff + pltpu.roll(both, 1, 0), 1, 1)
        field = (shifted_c - (both + pltpu.roll(diff, 1, 0))) * in_grid
        for n in range(strips):
            lanes = slice(n * LANES, (n + 1) * LANES)
            strip[n, g * rows : (g + 1) * rows, :] = field[:rows, lanes]
            strip[n, (dirs + 1) * rows + g : (dirs + 1) * rows + g + 1, :] = field[
                rows : rows + 1, lanes
            ]
    turned = {}
    lane = lane_index()

    def turn(n, by):
        if (n, by) not in turned:
            turned[n, by] = pltpu.roll(strip[n], (-by) % LANES, 1)
        return turned[n, by]

    for t in range(plan.tiles):
        begin = margin - plan.side + t * plan.own
        by = begin % LANES
        for n in range(plan.lane_tiles):
            at = begin // LANES + n
            if by == 0:
                out[t, n] = strip[at]
            else:
                near = tall(lane < LANES - by, plan.in_rows)
                out[t, n] = jnp.where(near, turn(at, by), turn(at + 1, by))


def solve_kernel(
    plan, place, offsets, weights, fields, out, q, keep, v0, v1, v2, phase, both, diff, smooth
):
    layers, dirs, rows = plan.layers, plan.dirs, plan.rows
    total, tiles = plan.grid_rows, range(plan.lane_tiles)
    chunk = total
    while chunk * plan.lane_tiles > 8 * 24:
        chunk //= 2
    starts = range(0, total, chunk)
    first = (place[0] * plan.tiles + place[1]) * plan.own - plan.side
    lane = lane_index()
    in_grid = []
    owned = []
    for t in tiles:
        local = lane + t * LANES
        column = local + first
        in_grid.append(
            tall(jnp.where((column >= 0) & (column < plan.width), 1.0, 0.0), chunk)
        )
        owned.append(tall((local >= plan.side) & (local < plan.side + plan.own), chunk))

    edge = jnp.zeros((PAD, LANES), jnp.float32)
    for t in tiles:
        for ref, count in ((q, dirs), (v0, layers), (v1, layers)):
            for i in range(count):
                ref[i, t, :PAD, :] = edge
                ref[i, t, PAD + total :, :] = edge
        for ref in (phase, both, diff, smooth):
            ref[t, :PAD, :] = edge
            ref[t, PAD + total :, :] = edge
        for s in range(plan.tiles):
            low = s * rows
            keep[t, low : low + rows, :] = fields[s, t, dirs * rows : (dirs + 1) * rows, :]
            for g in range(dirs):
                q[g, t, PAD + low : PAD + low + rows, :] = fields[s, t, g * rows : (g + 1) * rows, :]
        for s in range(1, plan.tiles):
            low = PAD + s * rows
            for g in range(dirs):
                carry = (dirs + 1) * rows + g
                q[g, t, low : low + 1, :] += fields[s - 1, t, carry : carry + 1, :]

    def back_project(layer, target, source):
        if source is not None:
            weight = weights[layer]
            for r in starts:
                x = [source[layer, t, PAD + r : PAD + r + chunk, :] for t in tiles]
                right = lane_shift(x, 1, chunk)
                left = lane_shift(x, -1, chunk)
                for t in tiles:
                    up = source[layer, t, PAD + r - 1 : PAD + r - 1 + chunk, :]
                    down = source[layer, t, PAD + r + 1 : PAD + r + 1 + chunk, :]
                    value = 4.0 * x[t] - up - down - left[t] - right[t]
                    smooth[t, PAD + r : PAD + r + chunk, :] = value * in_grid[t]
        for r in starts:
            sums = [jnp.zeros((chunk, LANES), jnp.float32) for _ in tiles]
            for g in range(dirs):
                at = (g * layers + layer) * 2
                low = PAD + r - offsets[at]
                moved = lane_shift(
                    [q[g, t, pl.ds(low, chunk), :] for t in tiles], -offsets[at + 1], chunk
                )
                sums = [sums[t] + moved[t] for t in tiles]
            sums = [0.5 * value for value in sums]
            if source is not None:
                x = [smooth[t, PAD + r : PAD + r + chunk, :] for t in tiles]
                right = lane_shift(x, 1, chunk)
                left = lane_shift(x, -1, chunk)
                for t in tiles:
                    up = smooth[t, PAD + r - 1 : PAD + r - 1 + chunk, :]
                    down = smooth[t, PAD + r + 1 : PAD + r + 1 + chunk, :]
                    value = 4.0 * x[t] - up - down - left[t] - right[t]
                    sums[t] = sums[t] + weight * value
            for t in tiles:
                target[layer, t, PAD + r : PAD + r + chunk, :] = sums[t] * in_grid[t]

    def project(g, source):
        for r in starts:
            sums = [jnp.zeros((chunk, LANES), jnp.float32) for _ in tiles]
            for layer in range(layers):
                at = (g * layers + layer) * 2
                low = PAD + r + offsets[at]
                moved = lane_shift(
                    [source[layer, t, pl.ds(low, chunk), :] for t in tiles], offsets[at + 1], chunk
                )
                sums = [sums[t] + moved[t] for t in tiles]
            for t in tiles:
                phase[t, PAD + r : PAD + r + chunk, :] = sums[t] * in_grid[t]
        for r in starts:
            p00 = [phase[t, PAD + r : PAD + r + chunk, :] for t in tiles]
            p10 = [phase[t, PAD + r + 1 : PAD + r + 1 + chunk, :] for t in tiles]
            p01 = lane_shift(p00, 1, chunk)
            p11 = lane_shift(p10, 1, chunk)
            for t in tiles:
                mask = keep[t, r : r + chunk, :]
                both[t, PAD + r : PAD + r + chunk, :] = mask * (p11[t] - p00[t])
                diff[t, PAD + r : PAD + r + chunk, :] = mask * (p01[t] - p10[t])
        for r in starts:
            here = slice(PAD + r, PAD + r + chunk)
            above = slice(PAD + r - 1, PAD + r - 1 + chunk)
            c = [diff[t, here, :] + both[t, above, :] for t in tiles]
            c = lane_shift(c, -1, chunk)
            for t in tiles:
                value = c[t] - (both[t, here, :] + diff[t, above, :])
                q[g, t, here, :] = value * in_grid[t]

    def each(count, body):
        def step(i, carry):
            body(i)
            return carry

        lax.fori_loop(0, count, step, 0)

    def fold(value):
        return jnp.sum(value.reshape(chunk // 8, 8, LANES), axis=0)

    def inner(terms, count):
        def step(layer, sums):
            for r in starts:
                for t in tiles:
                    pairs = terms(layer, t, slice(PAD + r, PAD + r + chunk))
                    sums = tuple(
                        s + fold(jnp.where(owned[t], value, 0.0)) for s, value in zip(sums, pairs)
                    )
            return sums

        zero = jnp.zeros((8, LANES), jnp.float32)
        sums = lax.fori_loop(0, layers, step, (zero,) * count)
        return [jnp.sum(s, keepdims=True) for s in sums]

    each(layers, lambda layer: back_project(layer, v0, None))
    each(dirs, lambda g: project(g, v0))
    each(layers, lambda layer: back_project(layer, v1, v0))

    def first_terms(layer, t, here):
        a, b = v0[layer, t, here, :], v1[layer, t, here, :]
        return a * a, a * b, b * b

    s00, s01, s11 = inner(first_terms, 3)
    coefficient = jnp.where(s11 > 0.0, s01 / jnp.where(s11 > 0.0, s11, 1.0), 0.0)
    each(dirs, lambda g: project(g, v1))
    each(layers, lambda layer: back_project(layer, v2, v1))
    spread = jnp.broadcast_to(coefficient, (chunk, LANES))

    def second_terms(layer, t, here):
        a, b, c = v0[layer, t, here, :], v1[layer, t, here, :], v2[layer, t, here, :]
        e = a - spread * b
        f = b - spread * c
        return e * e, e * b, e * f, e * c + b * f, b * c

    more = inner(second_terms, 5)
    scalars = [s00, s01, s11, coefficient] + more
    row = jnp.zeros((1, LANES), jnp.float32)
    for i, value in enumerate(scalars):
        row = jnp.where(lane[:1] == i, value, row)

    tail = 3 * plan.own_layers * rows
    note = jnp.broadcast_to(row[:, : plan.own], (plan.out_rows - tail, plan.own))
    keep_lanes = plan.side // LANES
    by = plan.side % LANES
    near = tall(lane < LANES - by, rows)
    for device in range(plan.layer_devices):
        for s in range(plan.tiles):
            to = device * plan.tiles + s
            for own in range(plan.own_layers):
                layer = device * plan.own_layers + own
                for i, ref in enumerate((v0, v1, v2)):
                    low = PAD + s * rows
                    block = [
                        pltpu.roll(ref[layer, t, low : low + rows, :], (-by) % LANES, 1)
                        for t in range(keep_lanes, plan.lane_tiles)
                    ]
                    pieces = []
                    for n in range(-(-plan.own // LANES)):
                        piece = block[n]
                        if n + 1 < len(block):
                            piece = jnp.where(near, piece, block[n + 1])
                        pieces.append(piece)
                    at = (own * 3 + i) * rows
                    for n, piece in enumerate(pieces):
                        size = min(LANES, plan.own - n * LANES)
                        out[to, at : at + rows, n * LANES : n * LANES + size] = piece[:, :size]
            out[to, tail:, :] = note


def coefficients(notes):
    s00, s01, s11, c, ee, eb, ef, mixed, bc = [notes[:, i : i + 1] for i in range(9)]

    def total(value):
        return jnp.sum(value, axis=0, keepdims=True)

    norm_0 = total(s00)
    power_0 = total(s01)
    alpha_0 = norm_0 / power_0
    delta = alpha_0 - c
    norm_1 = total(ee - 2.0 * delta * eb + delta * delta * s11)
    beta = norm_1 / norm_0
    power_1 = (
        total(ef - delta * mixed + delta * delta * bc)
        + 2.0 * beta * total(eb - delta * s11)
        + beta * beta * power_0
    )
    return alpha_0, beta, norm_1 / power_1


def outputs(a, b, c, scalars):
    alpha_0, beta, alpha_1 = scalars
    residual = a - alpha_0 * b
    image = b - alpha_0 * c
    estimate = alpha_0 * a + alpha_1 * (residual + beta * a)
    return estimate, residual - alpha_1 * (image + beta * b)


def combine_kernel(plan, blocks, estimate, residual):
    rows = plan.rows
    tail = 3 * plan.own_layers * rows
    scalars = coefficients(blocks[:, tail, :])
    scalars = [jnp.broadcast_to(value, (rows, plan.own)) for value in scalars]
    for k in range(plan.devices):
        for own in range(plan.own_layers):
            a, b, c = [
                blocks[k, (own * 3 + i) * rows : (own * 3 + i + 1) * rows, :] for i in range(3)
            ]
            x, r = outputs(a, b, c, scalars)
            estimate[own, :, k * plan.own : (k + 1) * plan.own] = x
            residual[own, :, k * plan.own : (k + 1) * plan.own] = r


def combine(plan, blocks):
    shape = (plan.own_layers, plan.rows, plan.width)
    if plan.own % LANES == 0:
        return pl.pallas_call(
            functools.partial(combine_kernel, plan),
            out_shape=[jax.ShapeDtypeStruct(shape, jnp.float32)] * 2,
            in_specs=[pl.BlockSpec(memory_space=VMEM)],
            out_specs=[pl.BlockSpec(memory_space=VMEM)] * 2,
            name="combine",
        )(blocks)
    tail = 3 * plan.own_layers * plan.rows
    scalars = coefficients(blocks[:, tail, :])
    fields = blocks[:, :tail].reshape(plan.devices, plan.own_layers, 3, plan.rows, plan.own)
    fields = fields.transpose(2, 1, 3, 0, 4).reshape((3,) + shape)
    return outputs(*fields, [value[0, 0] for value in scalars])


def per_device(mesh, measured_slopes, valid_mask, layer_offsets, reg_weight):
    dirs, _, rows, width = measured_slopes.shape
    plan = Plan(mesh, dirs, rows, width, reg_weight.shape[0])
    place = jnp.stack([lax.axis_index("layer"), lax.axis_index("tile")]).astype(jnp.int32)
    high = 16 * (-(-(rows + 1) // 16))
    strips = plan.strip // LANES
    sent = pl.pallas_call(
        functools.partial(gather_kernel, plan),
        out_shape=jax.ShapeDtypeStruct(
            (plan.tiles, plan.lane_tiles, plan.in_rows, LANES), jnp.float32
        ),
        in_specs=[
            pl.BlockSpec(memory_space=SMEM),
            pl.BlockSpec(memory_space=pl.ANY),
            pl.BlockSpec(memory_space=pl.ANY),
        ],
        out_specs=pl.BlockSpec(memory_space=VMEM),
        scratch_shapes=[
            pltpu.VMEM((dirs, 2, rows, plan.strip), jnp.float32),
            pltpu.VMEM((rows, plan.strip), jnp.int32),
            pltpu.VMEM((high, plan.strip), jnp.float32),
            pltpu.VMEM((high, plan.strip), jnp.float32),
            pltpu.VMEM((strips, plan.in_rows, LANES), jnp.float32),
            pltpu.SemaphoreType.DMA((2,)),
        ],
        name="gather",
    )(place, measured_slopes, valid_mask)
    fields = lax.all_to_all(sent, "tile", 0, 0)
    tall_rows = plan.grid_rows + 2 * PAD
    stack = pltpu.VMEM((plan.layers, plan.lane_tiles, tall_rows, LANES), jnp.float32)
    single = pltpu.VMEM((plan.lane_tiles, tall_rows, LANES), jnp.float32)
    blocks = pl.pallas_call(
        functools.partial(solve_kernel, plan),
        out_shape=jax.ShapeDtypeStruct((plan.devices, plan.out_rows, plan.own), jnp.float32),
        in_specs=[pl.BlockSpec(memory_space=SMEM)] * 3 + [pl.BlockSpec(memory_space=VMEM)],
        out_specs=pl.BlockSpec(memory_space=VMEM),
        scratch_shapes=[
            pltpu.VMEM((dirs, plan.lane_tiles, tall_rows, LANES), jnp.float32),
            pltpu.VMEM((plan.lane_tiles, plan.grid_rows, LANES), jnp.float32),
            stack,
            stack,
            stack,
            single,
            single,
            single,
            single,
        ],
        name="solve",
    )(place, layer_offsets.reshape(-1), reg_weight, fields)
    blocks = lax.all_to_all(blocks, ("layer", "tile"), 0, 0)
    return tuple(combine(plan, blocks))


def solution(mesh):
    return jax.shard_map(
        functools.partial(per_device, mesh),
        mesh=mesh,
        in_specs=(P(None, None, "tile", None), P("tile", None), P(), P()),
        out_specs=(P("layer", "tile", None), P("layer", "tile", None)),
        check_vma=False,
    )
```

time: 527 us -> 68.4 us (0.13)
  waiting for transfers between devices: 158 us -> 11.8 us
  blocking collectives: 153 us -> 22.1 us
  local copies, waits for them, and re-layouts: 104 us -> 9.98 us
  starting transfers between devices: 55.4 us -> 5.21 us
  other arithmetic: 35.5 us -> 0.64 us
  between operations: 18.8 us -> 0.65 us
  Pallas kernels: 0 us -> 17.6 us
    psum x3 -> x0, blocking collectives: 153 us -> none  [the longest x2 96.5 us: squares(): return lax.psum(jnp.sum(field * field), ('layer', 'tile'))]
    psum x2 -> x0, waiting for transfers between devices: 151 us -> none  [per_device(): apply_phase = lax.psum(total, 'layer')]
    gather x90 -> x0, local copies, waits for them, and re-layouts: 90.2 us -> none
    ppermute x16 -> x0, starting transfers between devices: 55.2 us -> none  [the longest x5 30.2 us: padded_2(): lax.ppermute(tail, axis, [(i, (i + 1) % count) for i in range(ends)])]
    all_to_all x0 -> x1, blocking collectives: none -> 22.1 us  [per_device(): blocks = lax.all_to_all(blocks, ('layer', 'tile'), 0, 0)]
    pallas_call x0 -> x3, Pallas kernels: none -> 17.6 us  [the longest x1 11.4 us: per_device(): pl.pallas_call(functools.partial(solve_kernel, plan), out_shape=jax.Shape...]
    mul x11 -> x0, other arithmetic: 13.2 us -> none  [the longest x3 3.41 us: per_device(): apply_slope_x = maskf * grad_x]
    all_to_all x0 -> x1, waiting for transfers between devices: none -> 11.8 us  [per_device(): fields = lax.all_to_all(sent, 'tile', 0, 0)]
  transfers between devices with their start and end apart: 18 -> 1, of which waited for: 11 -> 1; matrix products, arithmetic and copies ran while one was open for 1% -> 1% of each run, Pallas kernels for 0% -> 0%
where the time goes in v1:
time: 68.4 us; the launch traced here: 68 us
  blocking collectives  22.1 us (32%)
  Pallas kernels  17.6 us (26%)
  waiting for transfers between devices  11.8 us (17%)
  local copies, waits for them, and re-layouts  9.98 us (15%)
  starting transfers between devices  5.21 us (8%)
    all_to_all x1, blocking collectives, per_device(): blocks = lax.all_to_all(blocks, ('layer', 'tile'), 0, 0)  22.1 us
    all_to_all x1, waiting for transfers between devices, per_device(): fields = lax.all_to_all(sent, 'tile', 0, 0)  11.8 us
    pallas_call x1, Pallas kernels, per_device(): pl.pallas_call(functools.partial(solve_kernel, plan), out_shape=jax.Shape...  11.4 us
    unnamed x6, local copies, waits for them, and re-layouts  5.7 us
    all_to_all x1, starting transfers between devices, per_device(): fields = lax.all_to_all(sent, 'tile', 0, 0)  5.21 us
    pallas_call x1, Pallas kernels, per_device(): pl.pallas_call(functools.partial(gather_kernel, plan), out_shape=jax.Shap...  4.07 us
    pallas_call x2, local copies, waits for them, and re-layouts, combine(): pl.pallas_call(functools.partial(combine_kernel, plan), out_shape=[jax.Sh...  3.66 us
    pallas_call x1, Pallas kernels, combine(): pl.pallas_call(functools.partial(combine_kernel, plan), out_shape=[jax.Sh...  2.14 us
  transfers between devices with their start and end apart: 1, of which 1 were waited for; matrix products, arithmetic and copies ran while one was open for 1% of the time, Pallas kernels for 0%

profile of v1, /device:TPU:0, one launch (start us, length us, event | category | flops | bytes accessed | tf_op | source)
XLA Modules:
  0.0 68.0 jit_solution(7741487655505039829)
XLA Ops:
  0.6 4.7 %copy.11.slopes = f32[6,2,12,4096]{3,2,1,0:T(8,128)} copy(f32[6,2,12,4096]{3,1,2,0:T(2,128)} %param.4) | data formatting | bytes 4718592 | tf_op args[0]
  5.3 0.0 copy-start.1
  5.3 0.6 pad_add_fusion.place
  6.0 4.1 %gather.1 = f32[8,2,96,128]{3,2,1,0:T(8,128)} custom-call(s32[2]{0:T(128)} %pad_add_fusion.place, f32[6,2,12,4096]{3,2,1,0:T(8,128)} %copy.11.slopes, s32[12,4096]{1,0:T(8,128)} %mask.1), custom_call_target="tpu_custom_call" | custom-call | tf_op jit(solution)/shard_map/gather/pallas_call | solution.py:429
  10.1 5.2 %all-to-all-start = ((f32[8,2,96,128]{3,2,1,0:T(8,128)}), f32[8,2,96,128]{3,2,1,0:T(8,128)S(1)}, u32[]{:S(2)}, u32[]{:S(2)}) async-start(f32[8,2,96,128]{3,2,1,0:T(8,128)} %gather.1), calls=%async_computation | async-start | bytes 1572864 | tf_op jit(solution)/shard_map/all_to_all | solution.py:450
  15.3 0.0 copy-done.1
  15.3 0.1 copy.10
  15.4 0.6 reshape.7.offsets
  16.0 11.8 %all-to-all-done.fields = f32[8,2,96,128]{3,2,1,0:T(8,128)S(1)} async-done(((f32[8,2,96,128]{3,2,1,0:T(8,128)}), f32[8,2,96,128]{3,2,1,0:T(8,128)S(1)}, u32[]{:S(2)}, u32[]{:S(2)}) %all-to-all-start) | async-done | bytes 786464 | tf_op jit(solution)/shard_map/all_to_all | solution.py:450
  27.8 0.0 copy-start
  27.8 0.9 %copy-done = f32[8,2,96,128]{3,2,1,0:T(8,128)} copy-done((f32[8,2,96,128]{3,2,1,0:T(8,128)}, f32[8,2,96,128]{3,2,1,0:T(8,128)S(1)}, u32[]{:S(2)}) %copy-start) | copy-done | bytes 786456
  28.7 11.4 %solve.1 = f32[32,40,128]{2,1,0:T(8,128)} custom-call(s32[2]{0:T(128)} %pad_add_fusion.place, s32[48]{0:T(128)} %reshape.7.offsets, f32[4]{0:T(128)} %weights.1, f32[8,2,96,128]{3,2,1,0:T(8,128)} %copy-done), custom_call_target="tpu_custom_call" | custom-call | tf_op jit(solution)/shard_map/solve/pallas_call | solution.py:454
  40.1 22.1 %all_to_all.10.blocks = f32[32,40,128]{2,1,0:T(8,128)} all-to-all(f32[32,40,128]{2,1,0:T(8,128)} %solve.1), channel_id=1, replica_groups=mesh['layer'=4,'tile'=8] {'layer','tile'}, dimensions={0} | all-to-all | bytes 1310720 | tf_op jit(solution)/shard_map/all_to_all | solution.py:472
  62.2 2.1 %combine.1 = (f32[1,12,4096]{2,1,0:T(8,128)}, f32[1,12,4096]{2,1,0:T(8,128)}) custom-call(f32[32,40,128]{2,1,0:T(8,128)} %all_to_all.10.blocks), custom_call_target="tpu_custom_call" | custom-call | tf_op jit(solution)/shard_map/combine/pallas_call | solution.py:409
  64.3 1.8 %copy.12 = f32[1,12,4096]{2,0,1:T(1,128)} copy(f32[1,12,4096]{2,1,0:T(8,128)} %get-tuple-element.4) | data formatting | bytes 393216 | tf_op jit(solution)/shard_map/combine/pallas_call | solution.py:409
  66.1 1.8 %copy.13 = f32[1,12,4096]{2,0,1:T(1,128)} copy(f32[1,12,4096]{2,1,0:T(8,128)} %get-tuple-element.5) | data formatting | bytes 393216 | tf_op jit(solution)/shard_map/combine/pallas_call | solution.py:409
Async XLA Ops:
  5.3 9.9 %copy-start.1 = (s32[6,4,2]{0,2,1:T(2,128)S(1)}, s32[6,4,2]{0,2,1:T(2,128)}, u32[]{:S(2)}) copy-start(s32[6,4,2]{0,2,1:T(2,128)} %param.6) | copy-start | bytes 580
  10.1 17.8 %all-to-all-start = ((f32[8,2,96,128]{3,2,1,0:T(8,128)}), f32[8,2,96,128]{3,2,1,0:T(8,128)S(1)}, u32[]{:S(2)}, u32[]{:S(2)}) async-start(f32[8,2,96,128]{3,2,1,0:T(8,128)} %gather.1), calls=%async_computation | async-start | bytes 1572864 | tf_op jit(solution)/shard_map/all_to_all | solution.py:450
  27.8 0.9 %copy-start = (f32[8,2,96,128]{3,2,1,0:T(8,128)}, f32[8,2,96,128]{3,2,1,0:T(8,128)S(1)}, u32[]{:S(2)}) copy-start(f32[8,2,96,128]{3,2,1,0:T(8,128)S(1)} %all-to-all-done.fields) | copy-start | bytes 2359300

commit v2 on v1

v2 whole, which is shorter than its diff:
```python
import functools

import jax
import jax.numpy as jnp
from jax import lax
from jax.experimental import pallas as pl
from jax.experimental.pallas import tpu as pltpu
from jax.sharding import PartitionSpec as P

HALO = 8
LANES = 128
PAD = 8
REACH_ROW = 2 * (2 * HALO + 1)
REACH = REACH_ROW + HALO + 1
VMEM = pltpu.MemorySpace.VMEM
SMEM = pltpu.MemorySpace.SMEM


def round_up(value, unit):
    return -(-value // unit) * unit


class Plan:
    def __init__(self, mesh, dirs, rows, width, layers):
        self.layer_devices = mesh.shape["layer"]
        self.tiles = mesh.shape["tile"]
        self.devices = self.layer_devices * self.tiles
        self.dirs = dirs
        self.rows = rows
        self.width = width
        self.layers = layers
        self.own_layers = layers // self.layer_devices
        self.grid_rows = rows * self.tiles
        assert width % self.devices == 0 and layers % self.layer_devices == 0
        self.own = width // self.devices
        self.part = width // self.layer_devices
        assert self.part % LANES == 0
        self.lane_tiles = round_up(self.own + 2 * REACH, LANES) // LANES
        self.side = (self.lane_tiles * LANES - self.own) // 2
        self.margin = round_up(self.side + 1, LANES)
        self.strip = self.part + 2 * self.margin
        assert self.margin <= 4 * LANES and (2 * self.part // LANES) % 8 == 0
        self.raw_rows = 2 * self.part // LANES + 16
        self.high = round_up(rows + 1, 8)
        self.in_rows = round_up(dirs * (rows + 1) + rows, 8)
        self.out_rows = round_up(3 * self.own_layers * rows + 1, 8)
        self.chips = self.tiles // 2
        self.direct = self.tiles in (2, 4, 8) and self.own == LANES and self.lane_tiles == 2
        self.outs = self.chips if self.direct else 1
        self.sent_tiles = self.lane_tiles + 1 if self.direct else self.lane_tiles
        self.chunk = self.grid_rows
        while self.chunk * self.lane_tiles > 8 * 24:
            self.chunk //= 2


def in_vmem(value):
    return pltpu.with_memory_space_constraint(value, VMEM)


def lane_index():
    return lax.broadcasted_iota(jnp.int32, (8, LANES), 1)


def tall(mask, rows):
    return jnp.broadcast_to(mask[:1], (rows, LANES))


def lane_shift(tiles, steps, rows):
    count = len(tiles)
    if isinstance(steps, int):
        turn = (-steps) % LANES
    else:
        turn = jnp.where(steps > 0, LANES - steps, -steps)
    turned = [pltpu.roll(tile, turn, 1) for tile in tiles]
    if count == 1:
        return turned
    source = lane_index() + steps
    past = tall(source >= LANES, rows)
    before = tall(source < 0, rows)
    if count == 2:
        outside = past | before
        return [jnp.where(outside, turned[1 - t], turned[t]) for t in range(2)]
    return [
        jnp.where(
            past,
            turned[(t + 1) % count],
            jnp.where(before, turned[(t - 1) % count], turned[t]),
        )
        for t in range(count)
    ]


def place_of():
    return lax.axis_index("layer"), lax.axis_index("tile")


def gather_kernel(plan, slopes, mask, *refs):
    outs, (raw, raw_mask, strip, ready, sems, mask_sems) = refs[: plan.outs], refs[plan.outs :]
    layer, tile = place_of()
    rows, dirs, part = plan.rows, plan.dirs, plan.part
    last = plan.layer_devices - 1
    core = 2 * part // LANES
    start = pl.multiple_of(layer * core, 8)
    column = pl.multiple_of(layer * part, LANES)
    side = plan.margin

    def slope_copy(g, piece, source, size, target):
        return pltpu.make_async_copy(
            slopes.at[g, :, pl.ds(source, size), :],
            raw.at[g, pl.ds(0, rows), pl.ds(target, size), :],
            sems.at[g, piece],
        )

    def mask_copy(piece, source, size, target):
        return pltpu.make_async_copy(
            mask.at[:, pl.ds(source, size)],
            raw_mask.at[:, pl.ds(target, size)],
            mask_sems.at[piece],
        )

    def copies(piece):
        if piece == 0:
            return [mask_copy(0, column, part, side)] + [
                slope_copy(g, 0, start, core, 8) for g in range(dirs)
            ]
        if piece == 1:
            return [mask_copy(1, pl.multiple_of(column - side, LANES), side, 0)] + [
                slope_copy(g, 1, pl.multiple_of(start - 8, 8), 8, 0) for g in range(dirs)
            ]
        return [mask_copy(2, pl.multiple_of(column + part, LANES), side, side + part)] + [
            slope_copy(g, 2, pl.multiple_of(start + core, 8), 8, 8 + core) for g in range(dirs)
        ]

    def both_ways(act):
        for copy in copies(0):
            act(copy)

        @pl.when(layer > 0)
        def _():
            for copy in copies(1):
                act(copy)

        @pl.when(layer < last)
        def _():
            for copy in copies(2):
                act(copy)

    both_ways(lambda copy: copy.start())

    @pl.when(layer == 0)
    def _():
        raw_mask[:, :side] = jnp.zeros((rows, side), jnp.int32)

    @pl.when(layer == last)
    def _():
        raw_mask[:, side + part :] = jnp.zeros((rows, side), jnp.int32)

    both_ways(lambda copy: copy.wait())

    strips = plan.strip // LANES
    high = plan.high
    used = dirs * (rows + 1) + rows
    lane = lane_index()
    wrap = tall(lane == 0, high)
    blank = jnp.zeros((high - rows, LANES), jnp.float32)
    valid = []
    for n in range(strips):
        keep = raw_mask[:, n * LANES : (n + 1) * LANES].astype(jnp.float32)
        strip[n, dirs * rows : (dirs + 1) * rows, :] = keep
        if used < plan.in_rows:
            strip[n, used:, :] = jnp.zeros((plan.in_rows - used, LANES), jnp.float32)
        valid.append(jnp.concatenate([keep, blank], axis=0) > 0.0)
    for g in range(dirs):
        flat = raw.at[g].reshape(high * plan.raw_rows, LANES)
        before = None
        for n in range(strips):
            at = 2 * n + 8 - 2 * (side // LANES)
            slope_x = flat[pl.ds(at, high, stride=plan.raw_rows), :]
            slope_y = flat[pl.ds(at + 1, high, stride=plan.raw_rows), :]
            both = jnp.where(valid[n], slope_x + slope_y, 0.0)
            diff = jnp.where(valid[n], slope_x - slope_y, 0.0)
            c = pltpu.roll(diff + pltpu.roll(both, 1, 0), 1, 1)
            shifted = c if before is None else jnp.where(wrap, before, c)
            before = c
            field = shifted - (both + pltpu.roll(diff, 1, 0))
            if n >= strips - side // LANES:
                inside = column + n * LANES - side + lane < plan.width
                field = jnp.where(tall(inside, high), field, 0.0)
            strip[n, g * rows : (g + 1) * rows, :] = field[:rows]
            carry = (dirs + 1) * rows + g
            strip[n, carry : carry + 1, :] = field[rows : rows + 1]
    turned = {}

    def turn(n, by):
        if by == 0:
            return strip[n]
        for at in (n, n + 1):
            if (at, by) not in turned:
                turned[at, by] = pltpu.roll(strip[at], (-by) % LANES, 1)
        near = tall(lane < LANES - by, plan.in_rows)
        return jnp.where(near, turned[n, by], turned[n + 1, by])

    begin = plan.margin - plan.side
    if plan.direct:
        for n in range(2 * plan.chips + 1):
            ready[n] = turn(begin // LANES + n, begin % LANES)
        for k, out in enumerate(outs):
            at = 2 * ((tile // 2) ^ k)
            for n in range(plan.sent_tiles):
                out[n] = ready[at + n]
        return
    for t in range(plan.tiles):
        at = begin + t * plan.own
        for n in range(plan.lane_tiles):
            outs[0][t, n] = turn(at // LANES + n, at % LANES)


def solve_kernel(plan, offsets, weights, *refs):
    count = 2 * plan.outs if plan.direct else 1
    fields, (out, q, keep, v0, v1, phase, smooth, packed) = refs[:count], refs[count:]
    layers, dirs, rows = plan.layers, plan.dirs, plan.rows
    total, tiles = plan.grid_rows, range(plan.lane_tiles)
    chunk = plan.chunk
    starts = range(0, total, chunk)
    unrolled = len(starts) == 1
    layer_place, tile_place = place_of()
    first = (layer_place * plan.tiles + tile_place) * plan.own - plan.side
    lane = lane_index()
    in_grid = []
    owned = []
    for t in tiles:
        local = lane + t * LANES
        column = local + first
        in_grid.append(tall(jnp.where((column >= 0) & (column < plan.width), 1.0, 0.0), chunk))
        owned.append(tall((local >= plan.side) & (local < plan.side + plan.own), chunk))
    two = plan.lane_tiles == 2 and plan.own == LANES

    def pack(window):
        if two:
            return jnp.where(owned[1], window[1], window[0])
        value = jnp.where(owned[0], window[0], 0.0)
        for t in tiles[1:]:
            value = jnp.where(owned[t], window[t], value)
        return value

    def packed_shift(window, steps):
        if not two:
            return pack(lane_shift(window, steps, chunk))
        turn = jnp.where(steps > 0, LANES - steps, -steps)
        turned = [pltpu.roll(tile, turn, 1) for tile in window]
        source = lane + steps
        outside = (source >= LANES) | (source < 0)
        swap = tall(outside ^ (lane < plan.side), chunk)
        return jnp.where(swap, turned[1], turned[0])

    edge = jnp.zeros((PAD, LANES), jnp.float32)
    for t in tiles:
        for ref, count in ((q, dirs), (v0, layers), (v1, layers), (phase, dirs), (smooth, layers)):
            for i in range(count):
                for half in ([()] if ref is not phase else [(0,), (1,)]):
                    ref[(i,) + half + (t, slice(0, PAD))] = edge
                    ref[(i,) + half + (t, slice(PAD + total, PAD + total + PAD))] = edge
        keep[t, :PAD, :] = edge
        keep[t, PAD + total :, :] = edge
    sources = []
    if plan.direct:
        core = tile_place % 2
        for i, field in enumerate(fields):
            tile = 2 * ((tile_place // 2) ^ (i % plan.outs)) + (core if i < plan.outs else 1 - core)
            sources.append((tile, [field.at[core + t] for t in tiles]))
    else:
        for tile in range(plan.tiles):
            sources.append((tile, [fields[0].at[tile, t] for t in tiles]))
    for tile, windows in sources:
        here = pl.ds(PAD + tile * rows, rows)
        for t, window in enumerate(windows):
            keep[t, here, :] = window[dirs * rows : (dirs + 1) * rows, :]
            for g in range(dirs):
                q[g, t, here, :] = window[g * rows : (g + 1) * rows, :]
    for tile, windows in sources:
        below = pl.ds(PAD + (tile + 1) * rows, 1)
        counts = jnp.where(tile + 1 < plan.tiles, 1.0, 0.0)
        for t, window in enumerate(windows):
            for g in range(dirs):
                carry = (dirs + 1) * rows + g
                q[g, t, below, :] += window[carry : carry + 1, :] * counts

    def four(x, up, down, left, right):
        return 4.0 * x - (up + down) - (left + right)

    def back_project(layer, level):
        source = (None, v0, v1)[level]
        if source is not None:
            for r in starts:
                here = slice(PAD + r, PAD + r + chunk)
                x = [source[layer, t, here, :] for t in tiles]
                right = lane_shift(x, 1, chunk)
                left = lane_shift(x, -1, chunk)
                for t in tiles:
                    up = source[layer, t, PAD + r - 1 : PAD + r - 1 + chunk, :]
                    down = source[layer, t, PAD + r + 1 : PAD + r + 1 + chunk, :]
                    smooth[layer, t, here, :] = four(x[t], up, down, left[t], right[t]) * in_grid[t]
        for r in starts:
            here = slice(PAD + r, PAD + r + chunk)
            sums = None
            for g in range(dirs):
                at = (g * layers + layer) * 2
                low = PAD + r - offsets[at]
                window = [q[g, t, pl.ds(low, chunk), :] for t in tiles]
                if level == 2:
                    moved = [packed_shift(window, -offsets[at + 1])]
                else:
                    moved = lane_shift(window, -offsets[at + 1], chunk)
                sums = moved if sums is None else [s + m for s, m in zip(sums, moved)]
            sums = [0.5 * value for value in sums]
            if source is not None:
                weight = weights[layer]
                x = [smooth[layer, t, here, :] for t in tiles]
                right = lane_shift(x, 1, chunk)
                left = lane_shift(x, -1, chunk)
                lap = []
                for t in tiles:
                    up = smooth[layer, t, PAD + r - 1 : PAD + r - 1 + chunk, :]
                    down = smooth[layer, t, PAD + r + 1 : PAD + r + 1 + chunk, :]
                    lap.append(four(x[t], up, down, left[t], right[t]))
                if level == 2:
                    lap = [pack(lap)]
                sums = [s + weight * value for s, value in zip(sums, lap)]
            if level == 2:
                packed[2, layer, r : r + chunk, :] = sums[0]
                continue
            sums = [s * inside for s, inside in zip(sums, in_grid)]
            target = (v0, v1)[level]
            for t in tiles:
                target[layer, t, here, :] = sums[t]
            packed[level, layer, r : r + chunk, :] = pack(sums)

    def project(g, source):
        for r in starts:
            here = slice(PAD + r, PAD + r + chunk)
            sums = None
            for layer in range(layers):
                at = (g * layers + layer) * 2
                low = PAD + r + offsets[at]
                window = [source[layer, t, pl.ds(low, chunk), :] for t in tiles]
                moved = lane_shift(window, offsets[at + 1], chunk)
                sums = moved if sums is None else [s + m for s, m in zip(sums, moved)]
            sums = [s * inside for s, inside in zip(sums, in_grid)]
            right = lane_shift(sums, 1, chunk)
            for t in tiles:
                phase[g, 0, t, here, :] = sums[t]
                phase[g, 1, t, here, :] = right[t]
        for r in starts:
            here = slice(PAD + r, PAD + r + chunk)
            below = slice(PAD + r + 1, PAD + r + 1 + chunk)
            above = slice(PAD + r - 1, PAD + r - 1 + chunk)
            ahead, level = [], []
            for t in tiles:
                p00, p01 = phase[g, 0, t, here, :], phase[g, 1, t, here, :]
                p10, p11 = phase[g, 0, t, below, :], phase[g, 1, t, below, :]
                up0, up1 = phase[g, 0, t, above, :], phase[g, 1, t, above, :]
                mask, mask_up = keep[t, here, :], keep[t, above, :]
                ahead.append(mask * (p01 - p10) + mask_up * (p01 - up0))
                level.append(mask * (p11 - p00) + mask_up * (up1 - p00))
            ahead = lane_shift(ahead, -1, chunk)
            for t in tiles:
                q[g, t, here, :] = (ahead[t] - level[t]) * in_grid[t]

    def each(count, body):
        if unrolled:
            for i in range(count):
                body(i)
            return

        def step(i, carry):
            body(i)
            return carry

        lax.fori_loop(0, count, step, 0)

    def fold(value):
        return jnp.sum(value.reshape(chunk // 8, 8, LANES), axis=0)

    def inner(terms, count):
        sums = [jnp.zeros((8, LANES), jnp.float32)] * count

        def step(layer, sums):
            for r in starts:
                values = terms([packed.at[i, layer, r : r + chunk, :] for i in range(3)])
                sums = [s + fold(value) for s, value in zip(sums, values)]
            return tuple(sums)

        if unrolled:
            for layer in range(layers):
                sums = step(layer, sums)
        else:
            sums = lax.fori_loop(0, layers, step, tuple(sums))
        return [jnp.sum(s, keepdims=True) for s in sums]

    def first_terms(refs):
        a, b = refs[0][...], refs[1][...]
        return a * a, a * b, b * b

    each(layers, lambda layer: back_project(layer, 0))
    each(dirs, lambda g: project(g, v0))
    each(layers, lambda layer: back_project(layer, 1))
    s00, s01, s11 = inner(first_terms, 3)
    coefficient = jnp.where(s11 > 0.0, s01 / jnp.where(s11 > 0.0, s11, 1.0), 0.0)
    each(dirs, lambda g: project(g, v1))
    each(layers, lambda layer: back_project(layer, 2))
    spread = jnp.broadcast_to(coefficient, (chunk, LANES))

    def second_terms(refs):
        a, b, c = [ref[...] for ref in refs]
        e = a - spread * b
        f = b - spread * c
        return e * e, e * b, e * f, e * c + b * f, b * c

    scalars = [s00, s01, s11, coefficient] + inner(second_terms, 5)
    row = jnp.zeros((1, LANES), jnp.float32)
    for i, value in enumerate(scalars):
        row = jnp.where(lane[:1] == i, value, row)
    tail = 3 * plan.own_layers * rows
    note = jnp.broadcast_to(row[:, : plan.own], (plan.out_rows - tail, plan.own))
    for device in range(plan.layer_devices):
        for s in range(plan.tiles):
            to = device * plan.tiles + s
            for own in range(plan.own_layers):
                for i in range(3):
                    block = packed[i, device * plan.own_layers + own, s * rows : (s + 1) * rows, :]
                    if plan.own < LANES:
                        block = pltpu.roll(block, (-plan.side) % LANES, 1)[:, : plan.own]
                    at = (own * 3 + i) * rows
                    out[to, at : at + rows, :] = block
            out[to, tail:, :] = note


def coefficients(notes):
    s00, s01, s11, c, ee, eb, ef, mixed, bc = [notes[:, i : i + 1] for i in range(9)]

    def total(value):
        return jnp.sum(value, axis=0, keepdims=True)

    norm_0 = total(s00)
    power_0 = total(s01)
    alpha_0 = norm_0 / power_0
    delta = alpha_0 - c
    norm_1 = total(ee - 2.0 * delta * eb + delta * delta * s11)
    beta = norm_1 / norm_0
    power_1 = (
        total(ef - delta * mixed + delta * delta * bc)
        + 2.0 * beta * total(eb - delta * s11)
        + beta * beta * power_0
    )
    return alpha_0, beta, norm_1 / power_1


def outputs(a, b, c, scalars):
    alpha_0, beta, alpha_1 = scalars
    residual = a - alpha_0 * b
    image = b - alpha_0 * c
    estimate = alpha_0 * a + alpha_1 * (residual + beta * a)
    return estimate, residual - alpha_1 * (image + beta * b)


def combine_kernel(plan, blocks, estimate, residual):
    rows = plan.rows
    tail = 3 * plan.own_layers * rows
    scalars = coefficients(blocks[:, tail, :])
    scalars = [jnp.broadcast_to(value, (rows, LANES)) for value in scalars]
    for k in range(plan.devices):
        for own in range(plan.own_layers):
            a, b, c = [
                blocks[k, (own * 3 + i) * rows : (own * 3 + i + 1) * rows, :] for i in range(3)
            ]
            where = pl.ds(own * rows * plan.devices + k, rows, stride=plan.devices)
            for value, ref in zip(outputs(a, b, c, scalars), (estimate, residual)):
                ref[where, :] = pltpu.roll(value, (-plan.side) % LANES, 1)


def combine(plan, blocks):
    shape = (plan.own_layers, plan.rows, plan.width)
    if plan.own == LANES:
        lines = (plan.own_layers * plan.rows * plan.devices, LANES)
        results = pl.pallas_call(
            functools.partial(combine_kernel, plan),
            out_shape=[jax.ShapeDtypeStruct(lines, jnp.float32)] * 2,
            in_specs=[pl.BlockSpec(memory_space=VMEM)],
            out_specs=[pl.BlockSpec(memory_space=VMEM)] * 2,
            name="combine",
        )(in_vmem(blocks))
        return [value.reshape(shape) for value in results]
    tail = 3 * plan.own_layers * plan.rows
    scalars = coefficients(blocks[:, tail, :])
    fields = blocks[:, :tail].reshape(plan.devices, plan.own_layers, 3, plan.rows, plan.own)
    fields = fields.transpose(2, 1, 3, 0, 4).reshape((3,) + shape)
    return outputs(*fields, [value[0, 0] for value in scalars])


def per_device(mesh, measured_slopes, valid_mask, layer_offsets, reg_weight):
    dirs, _, rows, width = measured_slopes.shape
    plan = Plan(mesh, dirs, rows, width, reg_weight.shape[0])
    column_tiles = width // LANES
    slopes = measured_slopes.reshape(dirs, 2, rows, column_tiles, LANES)
    slopes = slopes.transpose(0, 2, 3, 1, 4).reshape(dirs, rows, 2 * column_tiles, LANES)
    strips = plan.strip // LANES
    piece = (plan.sent_tiles, plan.in_rows, LANES)
    lead = () if plan.direct else (plan.tiles,)
    sent = pl.pallas_call(
        functools.partial(gather_kernel, plan),
        out_shape=[jax.ShapeDtypeStruct(lead + piece, jnp.float32)] * plan.outs,
        in_specs=[pl.BlockSpec(memory_space=pl.ANY)] * 2,
        out_specs=[pl.BlockSpec(memory_space=VMEM)] * plan.outs,
        scratch_shapes=[
            pltpu.VMEM((dirs, plan.high, plan.raw_rows, LANES), jnp.float32),
            pltpu.VMEM((rows, plan.strip), jnp.int32),
            pltpu.VMEM((strips, plan.in_rows, LANES), jnp.float32),
            pltpu.VMEM((strips - 1, plan.in_rows, LANES), jnp.float32),
            pltpu.SemaphoreType.DMA((dirs, 3)),
            pltpu.SemaphoreType.DMA((3,)),
        ],
        name="gather",
    )(slopes, valid_mask)
    if plan.direct:
        fields = list(sent)
        for k in reversed(range(1, plan.outs)):
            fields[k] = lax.ppermute(sent[k], "tile", [(i, i ^ (2 * k)) for i in range(plan.tiles)])
        swap = [(i, i ^ 1) for i in range(plan.tiles)]
        fields = fields + [lax.ppermute(field, "tile", swap) for field in fields]
    else:
        fields = [lax.all_to_all(sent[0], "tile", 0, 0)]
    fields = [in_vmem(field) for field in fields]
    tall_rows = plan.grid_rows + 2 * PAD

    def scratch(*lead):
        return pltpu.VMEM(lead + (plan.lane_tiles, tall_rows, LANES), jnp.float32)

    blocks = pl.pallas_call(
        functools.partial(solve_kernel, plan),
        out_shape=jax.ShapeDtypeStruct((plan.devices, plan.out_rows, plan.own), jnp.float32),
        in_specs=[pl.BlockSpec(memory_space=SMEM)] * 2
        + [pl.BlockSpec(memory_space=VMEM)] * len(fields),
        out_specs=pl.BlockSpec(memory_space=VMEM),
        scratch_shapes=[
            scratch(dirs),
            scratch(),
            scratch(plan.layers),
            scratch(plan.layers),
            scratch(dirs, 2),
            scratch(plan.layers),
            pltpu.VMEM((3, plan.layers, plan.grid_rows, LANES), jnp.float32),
        ],
        name="solve",
    )(layer_offsets.reshape(-1), reg_weight, *fields)
    blocks = lax.all_to_all(blocks, ("layer", "tile"), 0, 0)
    return tuple(combine(plan, blocks))


def solution(mesh):
    return jax.shard_map(
        functools.partial(per_device, mesh),
        mesh=mesh,
        in_specs=(P(None, None, "tile", None), P("tile", None), P(), P()),
        out_specs=(P("layer", "tile", None), P("layer", "tile", None)),
        check_vma=False,
    )
```

time: 68.4 us -> 50.8 us (0.74)
  local copies, waits for them, and re-layouts: 9.98 us -> 1.64 us
  Pallas kernels: 17.6 us -> 12.8 us
  waiting for transfers between devices: 11.8 us -> 7.47 us
  blocking collectives: 22.1 us -> 23 us
    all_to_all x1 -> x0, waiting for transfers between devices: 11.8 us -> none  [per_device(): fields = lax.all_to_all(sent, 'tile', 0, 0)]
    ppermute x0 -> x7, waiting for transfers between devices: none -> 7.47 us  [the longest x3 7.13 us: per_device(): lax.ppermute(sent[k], 'tile', [(i, i ^ 2 * k) for i in range(plan.tiles)])]
    all_to_all x1 -> x0, starting transfers between devices: 5.21 us -> none  [per_device(): fields = lax.all_to_all(sent, 'tile', 0, 0)]
    ppermute x0 -> x7, starting transfers between devices: none -> 5.09 us  [the longest x3 4.57 us: per_device(): lax.ppermute(sent[k], 'tile', [(i, i ^ 2 * k) for i in range(plan.tiles)])]
    unnamed x6 -> x5, local copies, waits for them, and re-layouts: 5.7 us -> 1.02 us
    pallas_call x2 -> x0, local copies, waits for them, and re-layouts: 3.66 us -> none  [combine(): pl.pallas_call(functools.partial(combine_kernel, plan), out_shape=[jax.Sh...]
    pallas_call x1, Pallas kernels: 11.4 us -> 8.35 us  [per_device(): pl.pallas_call(functools.partial(solve_kernel, plan), out_shape=jax.Shape...]
    pallas_call x1, Pallas kernels: 4.07 us -> 3.06 us  [per_device(): pl.pallas_call(functools.partial(gather_kernel, plan), out_shape=[jax.Sha...]
  transfers between devices with their start and end apart: 1 -> 7, of which waited for: 1 -> 4; matrix products, arithmetic and copies ran while one was open for 1% -> 1% of each run, Pallas kernels for 0% -> 0%
where the time goes in v2:
time: 50.8 us; the launch traced here: 50.6 us
  blocking collectives  23 us (45%)
  Pallas kernels  12.8 us (25%)
  waiting for transfers between devices  7.47 us (15%)
  starting transfers between devices  5.09 us (10%)
  local copies, waits for them, and re-layouts  1.64 us (3%)
  between operations  0.66 us (1%)
    all_to_all x1, blocking collectives, per_device(): blocks = lax.all_to_all(blocks, ('layer', 'tile'), 0, 0)  23 us
    pallas_call x1, Pallas kernels, per_device(): pl.pallas_call(functools.partial(solve_kernel, plan), out_shape=jax.Shape...  8.35 us
    ppermute x3, waiting for transfers between devices, per_device(): lax.ppermute(sent[k], 'tile', [(i, i ^ 2 * k) for i in range(plan.tiles)])  7.13 us
    ppermute x3, starting transfers between devices, per_device(): lax.ppermute(sent[k], 'tile', [(i, i ^ 2 * k) for i in range(plan.tiles)])  4.57 us
    pallas_call x1, Pallas kernels, per_device(): pl.pallas_call(functools.partial(gather_kernel, plan), out_shape=[jax.Sha...  3.06 us
    pallas_call x1, Pallas kernels, combine(): pl.pallas_call(functools.partial(combine_kernel, plan), out_shape=[jax.Sh...  1.35 us
    unnamed x5, local copies, waits for them, and re-layouts  1.02 us
  transfers between devices with their start and end apart: 7, of which 4 were waited for; matrix products, arithmetic and copies ran while one was open for 1% of the time, Pallas kernels for 0%

profile of v2, /device:TPU:0, one launch (start us, length us, event | category | flops | bytes accessed | tf_op | source)
XLA Modules:
  0.0 50.6 jit_solution(7521025029297895789)
XLA Ops:
  0.6 0.0 copy-start.1
  0.6 3.1 %gather.1 = (f32[3,96,128]{2,1,0:T(8,128)}, f32[3,96,128]{2,1,0:T(8,128)}, f32[3,96,128]{2,1,0:T(8,128)}, f32[3,96,128]{2,1,0:T(8,128)}) custom-call(f32[6,12,64,128]{3,2,1,0:T(8,128)} %bitcast.7, s32[12,4096]{1,0:T(8,128)} %mask.1), custom_call_target="tpu_custom_call" | custom-call | tf_op jit(solution)/shard_map/gather/pallas_call | solution.py:509
  3.7 3.0 %collective-permute-start = (f32[3,96,128]{2,1,0:T(8,128)}, f32[3,96,128]{2,1,0:T(8,128)S(1)}, u32[]{:S(2)}, u32[]{:S(2)}) collective-permute-start(f32[3,96,128]{2,1,0:T(8,128)} %get-tuple-element.9), channel_id=1, source_target_pairs={{0,2},{1,3},{2,0},{3,1},{4,6},{5,7},{6,4},{7,5},{8,10},{9,11},{10,... | collective-permute-start | bytes 442376 | tf_op jit(solution)/shard_map/ppermute | solution.py:527
  6.7 1.5 %collective-permute-start.1 = (f32[3,96,128]{2,1,0:T(8,128)}, f32[3,96,128]{2,1,0:T(8,128)S(1)}, u32[]{:S(2)}, u32[]{:S(2)}) collective-permute-start(f32[3,96,128]{2,1,0:T(8,128)} %get-tuple-element.10), channel_id=1, source_target_pairs={{0,4},{1,5},{2,6},{3,7},{4,0},{5,1},{6,2},{7,3},{8,12},{9,13},{10,... | collective-permute-start | bytes 442376 | tf_op jit(solution)/shard_map/ppermute | solution.py:527
  8.3 0.0 collective-permute-start.2
  8.3 0.0 collective-permute-start.3
  8.3 3.0 %collective-permute-done.refs_1_ = f32[3,96,128]{2,1,0:T(8,128)S(1)} collective-permute-done((f32[3,96,128]{2,1,0:T(8,128)}, f32[3,96,128]{2,1,0:T(8,128)S(1)}, u32[]{:S(2)}, u32[]{:S(2)}) %collective-permute-start) | collective-permute-done | bytes 147488 | tf_op jit(solution)/shard_map/ppermute | solution.py:527
  11.3 0.0 collective-permute-start.4
  11.3 4.1 %collective-permute-done.1.refs_2_ = f32[3,96,128]{2,1,0:T(8,128)S(1)} collective-permute-done((f32[3,96,128]{2,1,0:T(8,128)}, f32[3,96,128]{2,1,0:T(8,128)S(1)}, u32[]{:S(2)}, u32[]{:S(2)}) %collective-permute-start.1) | collective-permute-done | bytes 147488 | tf_op jit(solution)/shard_map/ppermute | solution.py:527
  15.4 0.0 collective-permute-start.5
  15.4 0.0 collective-permute-done.2.refs_3_
  15.4 0.5 %collective-permute-start.6 = (f32[3,96,128]{2,1,0:T(8,128)S(1)}, f32[3,96,128]{2,1,0:T(8,128)S(1)}, u32[]{:S(2)}, u32[]{:S(2)}) collective-permute-start(f32[3,96,128]{2,1,0:T(8,128)S(1)} %collective-permute-done.2.refs_3_), channel_id=1, source_target_pairs={{0,1},{1,0},{2,3},{3,2},{4,5},{5,4},{6,7},{7,6},{8,9},{9,8},{10,11... | collective-permute-start | bytes 442376 | tf_op jit(solution)/shard_map/ppermute | solution.py:529
  15.9 0.0 copy-done.1
  15.9 0.1 copy.10
  16.0 0.6 %reshape.19.offsets = s32[48]{0:T(128)} reshape(s32[6,4,2]{2,1,0:T(4,128)S(1)} %copy.10) | data formatting | bytes 384 | tf_op jit(solution)/shard_map/reshape | solution.py:554
  16.7 0.0 collective-permute-done.3.refs_4_
  16.7 0.0 collective-permute-done.4.refs_5_
  16.7 0.1 collective-permute-done.5.refs_6_
  16.8 0.2 collective-permute-done.6.refs_7_
  17.0 0.0 copy-start
  17.0 0.9 %copy-done = f32[3,96,128]{2,1,0:T(8,128)S(1)} copy-done((f32[3,96,128]{2,1,0:T(8,128)S(1)}, f32[3,96,128]{2,1,0:T(8,128)}, u32[]{:S(2)}) %copy-start) | copy-done | bytes 147480
  17.9 8.4 %solve.1 = f32[32,40,128]{2,1,0:T(8,128)} custom-call(s32[48]{0:T(128)} %reshape.19.offsets, f32[4]{0:T(128)} %weights.1, f32[3,96,128]{2,1,0:T(8,128)S(1)} %copy-done, f32[3,96,128]{2,1,0:T(8,128)S(1)} %collective-permute-done.refs_1_, f32[3,96,128]{2,1,0:T(8,128)S(1)} %collective-permute-done.1.refs_2_, f32[3,96,128]{2,1,0:T(8,128)S(1)} %collective-permute-done.2.refs_3_, ...), custom_call_target="tpu_custom_call" | custom-call | tf_op jit(solution)/shard_map/solve/pallas_call | solution.py:538
  26.3 23.0 %all_to_all.5.blocks = f32[32,40,128]{2,1,0:T(8,128)S(1)} all-to-all(f32[32,40,128]{2,1,0:T(8,128)} %solve.1), channel_id=1, replica_groups=mesh['layer'=4,'tile'=8] {'layer','tile'}, dimensions={0} | all-to-all | bytes 1310720 | tf_op jit(solution)/shard_map/all_to_all | solution.py:555
  49.2 1.3 %combine.1 = (f32[384,128]{1,0:T(8,128)}, f32[384,128]{1,0:T(8,128)}) custom-call(f32[32,40,128]{2,1,0:T(8,128)S(1)} %all_to_all.5.blocks), custom_call_target="tpu_custom_call" | custom-call | tf_op jit(solution)/shard_map/combine/pallas_call | solution.py:485
Async XLA Ops:
  0.6 15.3 %copy-start.1 = (s32[6,4,2]{0,2,1:T(2,128)S(1)}, s32[6,4,2]{0,2,1:T(2,128)}, u32[]{:S(2)}) copy-start(s32[6,4,2]{0,2,1:T(2,128)} %param.6) | copy-start | bytes 580
  3.7 7.6 %collective-permute-start = (f32[3,96,128]{2,1,0:T(8,128)}, f32[3,96,128]{2,1,0:T(8,128)S(1)}, u32[]{:S(2)}, u32[]{:S(2)}) collective-permute-start(f32[3,96,128]{2,1,0:T(8,128)} %get-tuple-element.9), channel_id=1, source_target_pairs={{0,2},{1,3},{2,0},{3,1},{4,6},{5,7},{6,4},{7,5},{8,10},{9,11},{10,... | collective-permute-start | bytes 442376 | tf_op jit(solution)/shard_map/ppermute | solution.py:527
  6.7 8.7 %collective-permute-start.1 = (f32[3,96,128]{2,1,0:T(8,128)}, f32[3,96,128]{2,1,0:T(8,128)S(1)}, u32[]{:S(2)}, u32[]{:S(2)}) collective-permute-start(f32[3,96,128]{2,1,0:T(8,128)} %get-tuple-element.10), channel_id=1, source_target_pairs={{0,4},{1,5},{2,6},{3,7},{4,0},{5,1},{6,2},{7,3},{8,12},{9,13},{10,... | collective-permute-start | bytes 442376 | tf_op jit(solution)/shard_map/ppermute | solution.py:527
  8.3 7.2 %collective-permute-start.2 = (f32[3,96,128]{2,1,0:T(8,128)}, f32[3,96,128]{2,1,0:T(8,128)S(1)}, u32[]{:S(2)}, u32[]{:S(2)}) collective-permute-start(f32[3,96,128]{2,1,0:T(8,128)} %get-tuple-element.11), channel_id=1, source_target_pairs={{0,6},{1,7},{2,4},{3,5},{4,2},{5,3},{6,0},{7,1},{8,14},{9,15},{10,... | collective-permute-start | bytes 442376 | tf_op jit(solution)/shard_map/ppermute | solution.py:527
  8.3 8.4 %collective-permute-start.3 = (f32[3,96,128]{2,1,0:T(8,128)}, f32[3,96,128]{2,1,0:T(8,128)S(1)}, u32[]{:S(2)}, u32[]{:S(2)}) collective-permute-start(f32[3,96,128]{2,1,0:T(8,128)} %get-tuple-element.8.refs_0_), channel_id=1, source_target_pairs={{0,1},{1,0},{2,3},{3,2},{4,5},{5,4},{6,7},{7,6},{8,9},{9,8},{10,11... | collective-permute-start | bytes 442376 | tf_op jit(solution)/shard_map/ppermute | solution.py:529
  11.3 5.4 %collective-permute-start.4 = (f32[3,96,128]{2,1,0:T(8,128)S(1)}, f32[3,96,128]{2,1,0:T(8,128)S(1)}, u32[]{:S(2)}, u32[]{:S(2)}) collective-permute-start(f32[3,96,128]{2,1,0:T(8,128)S(1)} %collective-permute-done.refs_1_), channel_id=1, source_target_pairs={{0,1},{1,0},{2,3},{3,2},{4,5},{5,4},{6,7},{7,6},{8,9},{9,8},{10,11... | collective-permute-start | bytes 442376 | tf_op jit(solution)/shard_map/ppermute | solution.py:529
  15.4 1.4 %collective-permute-start.5 = (f32[3,96,128]{2,1,0:T(8,128)S(1)}, f32[3,96,128]{2,1,0:T(8,128)S(1)}, u32[]{:S(2)}, u32[]{:S(2)}) collective-permute-start(f32[3,96,128]{2,1,0:T(8,128)S(1)} %collective-permute-done.1.refs_2_), channel_id=1, source_target_pairs={{0,1},{1,0},{2,3},{3,2},{4,5},{5,4},{6,7},{7,6},{8,9},{9,8},{10,11... | collective-permute-start | bytes 442376 | tf_op jit(solution)/shard_map/ppermute | solution.py:529
  15.4 1.6 %collective-permute-start.6 = (f32[3,96,128]{2,1,0:T(8,128)S(1)}, f32[3,96,128]{2,1,0:T(8,128)S(1)}, u32[]{:S(2)}, u32[]{:S(2)}) collective-permute-start(f32[3,96,128]{2,1,0:T(8,128)S(1)} %collective-permute-done.2.refs_3_), channel_id=1, source_target_pairs={{0,1},{1,0},{2,3},{3,2},{4,5},{5,4},{6,7},{7,6},{8,9},{9,8},{10,11... | collective-permute-start | bytes 442376 | tf_op jit(solution)/shard_map/ppermute | solution.py:529
  17.0 0.9 %copy-start = (f32[3,96,128]{2,1,0:T(8,128)S(1)}, f32[3,96,128]{2,1,0:T(8,128)}, u32[]{:S(2)}) copy-start(f32[3,96,128]{2,1,0:T(8,128)} %get-tuple-element.8.refs_0_) | copy-start | bytes 442372

commit v3 on v2

--- a/solution.py
+++ b/solution.py
@@ -304,13 +304,12 @@
             here = slice(PAD + r, PAD + r + chunk)
             sums = None
             for g in range(dirs):
-                at = (g * layers + layer) * 2
-                low = PAD + r - offsets[at]
+                low = PAD + r - offsets[layer, 0, g]
                 window = [q[g, t, pl.ds(low, chunk), :] for t in tiles]
                 if level == 2:
-                    moved = [packed_shift(window, -offsets[at + 1])]
+                    moved = [packed_shift(window, -offsets[layer, 1, g])]
                 else:
-                    moved = lane_shift(window, -offsets[at + 1], chunk)
+                    moved = lane_shift(window, -offsets[layer, 1, g], chunk)
                 sums = moved if sums is None else [s + m for s, m in zip(sums, moved)]
             sums = [0.5 * value for value in sums]
             if source is not None:
@@ -340,10 +339,9 @@
             here = slice(PAD + r, PAD + r + chunk)
             sums = None
             for layer in range(layers):
-                at = (g * layers + layer) * 2
-                low = PAD + r + offsets[at]
+                low = PAD + r + offsets[layer, 0, g]
                 window = [source[layer, t, pl.ds(low, chunk), :] for t in tiles]
-                moved = lane_shift(window, offsets[at + 1], chunk)
+                moved = lane_shift(window, offsets[layer, 1, g], chunk)
                 sums = moved if sums is None else [s + m for s, m in zip(sums, moved)]
             sums = [s * inside for s, inside in zip(sums, in_grid)]
             right = lane_shift(sums, 1, chunk)
@@ -506,9 +504,10 @@
     strips = plan.strip // LANES
     piece = (plan.sent_tiles, plan.in_rows, LANES)
     lead = () if plan.direct else (plan.tiles,)
+    kind = pltpu.VMEM if plan.direct else jax.ShapeDtypeStruct
     sent = pl.pallas_call(
         functools.partial(gather_kernel, plan),
-        out_shape=[jax.ShapeDtypeStruct(lead + piece, jnp.float32)] * plan.outs,
+        out_shape=[kind(lead + piece, jnp.float32)] * plan.outs,
         in_specs=[pl.BlockSpec(memory_space=pl.ANY)] * 2,
         out_specs=[pl.BlockSpec(memory_space=VMEM)] * plan.outs,
         scratch_shapes=[
@@ -537,7 +536,7 @@
 
     blocks = pl.pallas_call(
         functools.partial(solve_kernel, plan),
-        out_shape=jax.ShapeDtypeStruct((plan.devices, plan.out_rows, plan.own), jnp.float32),
+        out_shape=kind((plan.devices, plan.out_rows, plan.own), jnp.float32),
         in_specs=[pl.BlockSpec(memory_space=SMEM)] * 2
         + [pl.BlockSpec(memory_space=VMEM)] * len(fields),
         out_specs=pl.BlockSpec(memory_space=VMEM),
@@ -551,7 +550,7 @@
             pltpu.VMEM((3, plan.layers, plan.grid_rows, LANES), jnp.float32),
         ],
         name="solve",
-    )(layer_offsets.reshape(-1), reg_weight, *fields)
+    )(layer_offsets.transpose(1, 2, 0), reg_weight, *fields)
     blocks = lax.all_to_all(blocks, ("layer", "tile"), 0, 0)
     return tuple(combine(plan, blocks))
 

time: 50.8 us -> 47.9 us (0.943)
  local copies, waits for them, and re-layouts: 1.64 us -> 0 us
  Pallas kernels: 12.8 us -> 11.2 us
  waiting for transfers between devices: 7.47 us -> 7.99 us
    pallas_call x2, Pallas kernels: 11.4 us -> 9.84 us  [the longest x1 7.55 us: per_device(): pl.pallas_call(functools.partial(solve_kernel, plan), out_shape=kind((pla...]
    unnamed x5 -> x0, local copies, waits for them, and re-layouts: 1.02 us -> none
    ppermute x4, waiting for transfers between devices: 0.34 us -> 1.07 us  [per_device(): fields = fields + [lax.ppermute(field, 'tile', swap) for field in fields]]
    reshape x1 -> x0, local copies, waits for them, and re-layouts: 0.62 us -> none  [per_device(): layer_offsets.reshape(-1)]
  transfers between devices with their start and end apart: 7 -> 7, of which waited for: 4 -> 4; matrix products, arithmetic and copies ran while one was open for 1% -> 0% of each run, Pallas kernels for 0% -> 0%
where the time goes in v3:
time: 47.9 us; the launch traced here: 47.7 us
  blocking collectives  22.8 us (48%)
  Pallas kernels  11.2 us (23%)
  waiting for transfers between devices  7.99 us (17%)
  starting transfers between devices  5.09 us (11%)
  between operations  0.65 us (1%)
    all_to_all x1, blocking collectives, per_device(): blocks = lax.all_to_all(blocks, ('layer', 'tile'), 0, 0)  22.8 us
    pallas_call x1, Pallas kernels, per_device(): pl.pallas_call(functools.partial(solve_kernel, plan), out_shape=kind((pla...  7.55 us
    ppermute x3, waiting for transfers between devices, per_device(): lax.ppermute(sent[k], 'tile', [(i, i ^ 2 * k) for i in range(plan.tiles)])  6.92 us
    ppermute x3, starting transfers between devices, per_device(): lax.ppermute(sent[k], 'tile', [(i, i ^ 2 * k) for i in range(plan.tiles)])  4.57 us
    pallas_call x1, Pallas kernels, per_device(): pl.pallas_call(functools.partial(gather_kernel, plan), out_shape=[kind(le...  2.29 us
    pallas_call x1, Pallas kernels, combine(): pl.pallas_call(functools.partial(combine_kernel, plan), out_shape=[jax.Sh...  1.35 us
    ppermute x4, waiting for transfers between devices, per_device(): fields = fields + [lax.ppermute(field, 'tile', swap) for field in fields]  1.07 us
  transfers between devices with their start and end apart: 7, of which 4 were waited for; matrix products, arithmetic and copies ran while one was open for 0% of the time, Pallas kernels for 0%

profile of v3, /device:TPU:0, one launch (start us, length us, event | category | flops | bytes accessed | tf_op | source)
XLA Modules:
  0.0 47.7 jit_solution(17487957020218332334)
XLA Ops:
  0.6 2.3 %gather.1 = (f32[3,96,128]{2,1,0:T(8,128)S(1)}, f32[3,96,128]{2,1,0:T(8,128)S(1)}, f32[3,96,128]{2,1,0:T(8,128)S(1)}, f32[3,96,128]{2,1,0:T(8,128)S(1)}) custom-call(f32[6,12,64,128]{3,2,1,0:T(8,128)} %bitcast.8, s32[12,4096]{1,0:T(8,128)} %mask.1), custom_call_target="tpu_custom_call" | custom-call | tf_op jit(solution)/shard_map/gather/pallas_call | solution.py:508
  2.9 3.0 %collective-permute-start = (f32[3,96,128]{2,1,0:T(8,128)S(1)}, f32[3,96,128]{2,1,0:T(8,128)S(1)}, u32[]{:S(2)}, u32[]{:S(2)}) collective-permute-start(f32[3,96,128]{2,1,0:T(8,128)S(1)} %get-tuple-element.9), channel_id=1, source_target_pairs={{0,2},{1,3},{2,0},{3,1},{4,6},{5,7},{6,4},{7,5},{8,10},{9,11},{10,... | collective-permute-start | bytes 442376 | tf_op jit(solution)/shard_map/ppermute | solution.py:526
  6.0 1.5 %collective-permute-start.1 = (f32[3,96,128]{2,1,0:T(8,128)S(1)}, f32[3,96,128]{2,1,0:T(8,128)S(1)}, u32[]{:S(2)}, u32[]{:S(2)}) collective-permute-start(f32[3,96,128]{2,1,0:T(8,128)S(1)} %get-tuple-element.10), channel_id=1, source_target_pairs={{0,4},{1,5},{2,6},{3,7},{4,0},{5,1},{6,2},{7,3},{8,12},{9,13},{10,... | collective-permute-start | bytes 442376 | tf_op jit(solution)/shard_map/ppermute | solution.py:526
  7.5 0.0 collective-permute-start.2
  7.5 0.0 collective-permute-start.3
  7.5 2.8 %collective-permute-done.refs_1_ = f32[3,96,128]{2,1,0:T(8,128)S(1)} collective-permute-done((f32[3,96,128]{2,1,0:T(8,128)S(1)}, f32[3,96,128]{2,1,0:T(8,128)S(1)}, u32[]{:S(2)}, u32[]{:S(2)}) %collective-permute-start) | collective-permute-done | bytes 147488 | tf_op jit(solution)/shard_map/ppermute | solution.py:526
  10.3 0.0 collective-permute-start.4
  10.3 4.1 %collective-permute-done.1.refs_2_ = f32[3,96,128]{2,1,0:T(8,128)S(1)} collective-permute-done((f32[3,96,128]{2,1,0:T(8,128)S(1)}, f32[3,96,128]{2,1,0:T(8,128)S(1)}, u32[]{:S(2)}, u32[]{:S(2)}) %collective-permute-start.1) | collective-permute-done | bytes 147488 | tf_op jit(solution)/shard_map/ppermute | solution.py:526
  14.4 0.0 collective-permute-start.5
  14.4 0.0 collective-permute-done.2.refs_3_
  14.4 0.5 %collective-permute-start.6 = (f32[3,96,128]{2,1,0:T(8,128)S(1)}, f32[3,96,128]{2,1,0:T(8,128)S(1)}, u32[]{:S(2)}, u32[]{:S(2)}) collective-permute-start(f32[3,96,128]{2,1,0:T(8,128)S(1)} %collective-permute-done.2.refs_3_), channel_id=1, source_target_pairs={{0,1},{1,0},{2,3},{3,2},{4,5},{5,4},{6,7},{7,6},{8,9},{9,8},{10,11... | collective-permute-start | bytes 442376 | tf_op jit(solution)/shard_map/ppermute | solution.py:528
  14.9 0.0 collective-permute-done.3.refs_4_
  14.9 0.0 collective-permute-done.4.refs_5_
  14.9 0.9 %collective-permute-done.5.refs_6_ = f32[3,96,128]{2,1,0:T(8,128)S(1)} collective-permute-done((f32[3,96,128]{2,1,0:T(8,128)S(1)}, f32[3,96,128]{2,1,0:T(8,128)S(1)}, u32[]{:S(2)}, u32[]{:S(2)}) %collective-permute-start.5) | collective-permute-done | bytes 147488 | tf_op jit(solution)/shard_map/ppermute | solution.py:528
  15.8 0.2 collective-permute-done.6.refs_7_
  16.0 7.6 %solve.1 = f32[32,40,128]{2,1,0:T(8,128)S(1)} custom-call(s32[4,2,6]{2,1,0:T(2,128)} %bitcast.9, f32[4]{0:T(128)} %weights.1, f32[3,96,128]{2,1,0:T(8,128)S(1)} %get-tuple-element.8.refs_0_, f32[3,96,128]{2,1,0:T(8,128)S(1)} %collective-permute-done.refs_1_, f32[3,96,128]{2,1,0:T(8,128)S(1)} %collective-permute-done.1.refs_2_, ...), custom_call_target="tpu_custom_call" | custom-call | tf_op jit(solution)/shard_map/solve/pallas_call | solution.py:537
  23.6 22.8 %all_to_all.5.blocks = f32[32,40,128]{2,1,0:T(8,128)S(1)} all-to-all(f32[32,40,128]{2,1,0:T(8,128)S(1)} %solve.1), channel_id=1, replica_groups=mesh['layer'=4,'tile'=8] {'layer','tile'}, dimensions={0} | all-to-all | bytes 1310720 | tf_op jit(solution)/shard_map/all_to_all | solution.py:554
  46.3 1.3 %combine.1 = (f32[384,128]{1,0:T(8,128)}, f32[384,128]{1,0:T(8,128)}) custom-call(f32[32,40,128]{2,1,0:T(8,128)S(1)} %all_to_all.5.blocks), custom_call_target="tpu_custom_call" | custom-call | tf_op jit(solution)/shard_map/combine/pallas_call | solution.py:483
Async XLA Ops:
  2.9 7.4 %collective-permute-start = (f32[3,96,128]{2,1,0:T(8,128)S(1)}, f32[3,96,128]{2,1,0:T(8,128)S(1)}, u32[]{:S(2)}, u32[]{:S(2)}) collective-permute-start(f32[3,96,128]{2,1,0:T(8,128)S(1)} %get-tuple-element.9), channel_id=1, source_target_pairs={{0,2},{1,3},{2,0},{3,1},{4,6},{5,7},{6,4},{7,5},{8,10},{9,11},{10,... | collective-permute-start | bytes 442376 | tf_op jit(solution)/shard_map/ppermute | solution.py:526
  6.0 8.5 %collective-permute-start.1 = (f32[3,96,128]{2,1,0:T(8,128)S(1)}, f32[3,96,128]{2,1,0:T(8,128)S(1)}, u32[]{:S(2)}, u32[]{:S(2)}) collective-permute-start(f32[3,96,128]{2,1,0:T(8,128)S(1)} %get-tuple-element.10), channel_id=1, source_target_pairs={{0,4},{1,5},{2,6},{3,7},{4,0},{5,1},{6,2},{7,3},{8,12},{9,13},{10,... | collective-permute-start | bytes 442376 | tf_op jit(solution)/shard_map/ppermute | solution.py:526
  7.5 7.0 %collective-permute-start.2 = (f32[3,96,128]{2,1,0:T(8,128)S(1)}, f32[3,96,128]{2,1,0:T(8,128)S(1)}, u32[]{:S(2)}, u32[]{:S(2)}) collective-permute-start(f32[3,96,128]{2,1,0:T(8,128)S(1)} %get-tuple-element.11), channel_id=1, source_target_pairs={{0,6},{1,7},{2,4},{3,5},{4,2},{5,3},{6,0},{7,1},{8,14},{9,15},{10,... | collective-permute-start | bytes 442376 | tf_op jit(solution)/shard_map/ppermute | solution.py:526
  7.5 7.4 %collective-permute-start.3 = (f32[3,96,128]{2,1,0:T(8,128)S(1)}, f32[3,96,128]{2,1,0:T(8,128)S(1)}, u32[]{:S(2)}, u32[]{:S(2)}) collective-permute-start(f32[3,96,128]{2,1,0:T(8,128)S(1)} %get-tuple-element.8.refs_0_), channel_id=1, source_target_pairs={{0,1},{1,0},{2,3},{3,2},{4,5},{5,4},{6,7},{7,6},{8,9},{9,8},{10,11... | collective-permute-start | bytes 442376 | tf_op jit(solution)/shard_map/ppermute | solution.py:528
  10.3 4.6 %collective-permute-start.4 = (f32[3,96,128]{2,1,0:T(8,128)S(1)}, f32[3,96,128]{2,1,0:T(8,128)S(1)}, u32[]{:S(2)}, u32[]{:S(2)}) collective-permute-start(f32[3,96,128]{2,1,0:T(8,128)S(1)} %collective-permute-done.refs_1_), channel_id=1, source_target_pairs={{0,1},{1,0},{2,3},{3,2},{4,5},{5,4},{6,7},{7,6},{8,9},{9,8},{10,11... | collective-permute-start | bytes 442376 | tf_op jit(solution)/shard_map/ppermute | solution.py:528
  14.4 1.4 %collective-permute-start.5 = (f32[3,96,128]{2,1,0:T(8,128)S(1)}, f32[3,96,128]{2,1,0:T(8,128)S(1)}, u32[]{:S(2)}, u32[]{:S(2)}) collective-permute-start(f32[3,96,128]{2,1,0:T(8,128)S(1)} %collective-permute-done.1.refs_2_), channel_id=1, source_target_pairs={{0,1},{1,0},{2,3},{3,2},{4,5},{5,4},{6,7},{7,6},{8,9},{9,8},{10,11... | collective-permute-start | bytes 442376 | tf_op jit(solution)/shard_map/ppermute | solution.py:528
  14.4 1.6 %collective-permute-start.6 = (f32[3,96,128]{2,1,0:T(8,128)S(1)}, f32[3,96,128]{2,1,0:T(8,128)S(1)}, u32[]{:S(2)}, u32[]{:S(2)}) collective-permute-start(f32[3,96,128]{2,1,0:T(8,128)S(1)} %collective-permute-done.2.refs_3_), channel_id=1, source_target_pairs={{0,1},{1,0},{2,3},{3,2},{4,5},{5,4},{6,7},{7,6},{8,9},{9,8},{10,11... | collective-permute-start | bytes 442376 | tf_op jit(solution)/shard_map/ppermute | solution.py:528

commit v4 on v3

v4 whole, which is shorter than its diff:
```python
import functools

import jax
import jax.numpy as jnp
from jax import lax
from jax.experimental import pallas as pl
from jax.experimental.pallas import tpu as pltpu
from jax.sharding import PartitionSpec as P

HALO = 8
LANES = 128
PAD = 8
REACH_ROW = 2 * (2 * HALO + 1)
REACH = REACH_ROW + HALO + 1
VMEM = pltpu.MemorySpace.VMEM
SMEM = pltpu.MemorySpace.SMEM


def round_up(value, unit):
    return -(-value // unit) * unit


class Plan:
    def __init__(self, mesh, dirs, rows, width, layers):
        self.layer_devices = mesh.shape["layer"]
        self.tiles = mesh.shape["tile"]
        self.devices = self.layer_devices * self.tiles
        self.dirs = dirs
        self.rows = rows
        self.width = width
        self.layers = layers
        self.own_layers = layers // self.layer_devices
        self.grid_rows = rows * self.tiles
        assert width % self.devices == 0 and layers % self.layer_devices == 0
        self.own = width // self.devices
        self.part = width // self.layer_devices
        assert self.part % LANES == 0
        self.lane_tiles = round_up(self.own + 2 * REACH, LANES) // LANES
        self.side = (self.lane_tiles * LANES - self.own) // 2
        self.margin = round_up(self.side + 1, LANES)
        self.strip = self.part + 2 * self.margin
        assert self.margin <= 4 * LANES and (2 * self.part // LANES) % 8 == 0
        self.raw_core = min(2 * self.part // LANES + 16, 2 * width // LANES)
        self.raw_rows = 2 * self.part // LANES + 32
        assert self.strip <= width
        self.high = round_up(rows + 1, 8)
        self.used_rows = dirs * (rows + 1) + rows
        self.in_rows = round_up(self.used_rows, 8)
        self.out_rows = round_up(3 * self.own_layers * rows + 1, 8)
        self.chips = self.tiles // 2
        self.direct = self.tiles in (2, 4, 8) and self.own == LANES and self.lane_tiles == 2
        self.outs = self.chips if self.direct else 1
        self.sent_tiles = self.lane_tiles + 1 if self.direct else self.lane_tiles
        self.chunk = self.grid_rows
        while self.chunk > (96 if self.direct else 192):
            self.chunk //= 2


def in_vmem(value):
    return pltpu.with_memory_space_constraint(value, VMEM)


def lane_index():
    return lax.broadcasted_iota(jnp.int32, (8, LANES), 1)


def tall(mask, rows):
    return jnp.broadcast_to(mask[:1], (rows, LANES))


def lane_shift(tiles, steps, rows):
    count = len(tiles)
    if isinstance(steps, int):
        turn = (-steps) % LANES
    else:
        turn = jnp.where(steps > 0, LANES - steps, -steps)
    turned = [pltpu.roll(tile, turn, 1) for tile in tiles]
    if count == 1:
        return turned
    source = lane_index() + steps
    past = tall(source >= LANES, rows)
    before = tall(source < 0, rows)
    if count == 2:
        outside = past | before
        return [jnp.where(outside, turned[1 - t], turned[t]) for t in range(2)]
    return [
        jnp.where(
            past,
            turned[(t + 1) % count],
            jnp.where(before, turned[(t - 1) % count], turned[t]),
        )
        for t in range(count)
    ]


def place_of():
    return lax.axis_index("layer"), lax.axis_index("tile")


def gather_kernel(plan, slopes, mask, *refs):
    outs, (raw, raw_mask, strip, ready, sems) = refs[: plan.outs], refs[plan.outs :]
    layer, tile = place_of()
    rows, dirs, part, width = plan.rows, plan.dirs, plan.part, plan.width
    side = plan.margin
    column = layer * part - side
    line = 2 * (layer * part // LANES)
    base = jnp.clip(column, 0, width - plan.strip)
    base_line = jnp.clip(line - 8, 0, 2 * width // LANES - plan.raw_core)
    slope_copies = [
        pltpu.make_async_copy(
            slopes.at[g, :, pl.ds(pl.multiple_of(base_line, 8), plan.raw_core), :],
            raw.at[g, pl.ds(0, rows), pl.ds(8, plan.raw_core), :],
            sems.at[g],
        )
        for g in range(dirs)
    ]
    mask_copy = pltpu.make_async_copy(
        mask.at[:, pl.ds(pl.multiple_of(base, LANES), plan.strip)], raw_mask, sems.at[dirs]
    )
    mask_copy.start()
    for copy in slope_copies:
        copy.start()
    mask_copy.wait()

    strips = plan.strip // LANES
    high = plan.high
    used = dirs * (rows + 1) + rows
    lane = lane_index()
    wrap = tall(lane == 0, high)
    blank = jnp.zeros((high - rows, LANES), jnp.float32)
    valid = []
    for n in range(strips):
        at = jnp.clip(column + n * LANES - base, 0, plan.strip - LANES)
        here = raw_mask[:, pl.ds(pl.multiple_of(at, LANES), LANES)].astype(jnp.float32)
        begin = column + n * LANES
        keep = jnp.where((begin >= 0) & (begin < width), here, 0.0)
        strip[n, dirs * rows : (dirs + 1) * rows, :] = keep
        if used < plan.in_rows:
            strip[n, used:, :] = jnp.zeros((plan.in_rows - used, LANES), jnp.float32)
        valid.append(keep > 0.0)
    for g in range(dirs):
        slope_copies[g].wait()
        flat = raw.at[g].reshape(high * plan.raw_rows, LANES)
        before = None
        for n in range(strips):
            at = line - base_line + 2 * n + 8 - 2 * (side // LANES)
            slope_x = flat[pl.ds(at, rows, stride=plan.raw_rows), :]
            slope_y = flat[pl.ds(at + 1, rows, stride=plan.raw_rows), :]
            both = jnp.concatenate([jnp.where(valid[n], slope_x + slope_y, 0.0), blank], axis=0)
            diff = jnp.concatenate([jnp.where(valid[n], slope_x - slope_y, 0.0), blank], axis=0)
            c = pltpu.roll(diff + pltpu.roll(both, 1, 0), 1, 1)
            shifted = c if before is None else jnp.where(wrap, before, c)
            before = c
            field = shifted - (both + pltpu.roll(diff, 1, 0))
            if n >= strips - side // LANES:
                inside = column + n * LANES + lane < width
                field = jnp.where(tall(inside, high), field, 0.0)
            strip[n, g * rows : (g + 1) * rows, :] = field[:rows]
            carry = (dirs + 1) * rows + g
            strip[n, carry : carry + 1, :] = field[rows : rows + 1]
    turned = {}

    def turn(n, by):
        if by == 0:
            return strip[n]
        for at in (n, n + 1):
            if (at, by) not in turned:
                turned[at, by] = pltpu.roll(strip[at], (-by) % LANES, 1)
        near = tall(lane < LANES - by, plan.in_rows)
        return jnp.where(near, turned[n, by], turned[n + 1, by])

    begin = plan.margin - plan.side
    if plan.direct:
        for n in range(2 * plan.chips + 1):
            ready[n] = turn(begin // LANES + n, begin % LANES)
        for k, out in enumerate(outs):
            at = 2 * ((tile // 2) ^ k)
            for n in range(plan.sent_tiles):
                out[plan.used_rows * n : plan.used_rows * (n + 1), :] = ready[
                    at + n, : plan.used_rows, :
                ]
        return
    for t in range(plan.tiles):
        at = begin + t * plan.own
        for n in range(plan.lane_tiles):
            outs[0][t, n] = turn(at // LANES + n, at % LANES)


def solve_kernel(plan, offsets, weights, *refs):
    count = 2 * plan.outs if plan.direct else 1
    fields, (out, q, keep, v0, v1, phase, smooth, packed) = refs[:count], refs[count:]
    layers, dirs, rows = plan.layers, plan.dirs, plan.rows
    total, tiles = plan.grid_rows, range(plan.lane_tiles)
    chunk = plan.chunk
    starts = range(0, total, chunk)
    unrolled = plan.direct
    layer_place, tile_place = place_of()
    first = (layer_place * plan.tiles + tile_place) * plan.own - plan.side
    lane = lane_index()
    in_grid = []
    owned = []
    for t in tiles:
        local = lane + t * LANES
        column = local + first
        in_grid.append(tall(jnp.where((column >= 0) & (column < plan.width), 1.0, 0.0), chunk))
        owned.append(tall((local >= plan.side) & (local < plan.side + plan.own), chunk))
    two = plan.lane_tiles == 2 and plan.own == LANES

    def pack(window):
        if two:
            return jnp.where(owned[1], window[1], window[0])
        value = jnp.where(owned[0], window[0], 0.0)
        for t in tiles[1:]:
            value = jnp.where(owned[t], window[t], value)
        return value

    def packed_shift(window, steps):
        if not two:
            return pack(lane_shift(window, steps, chunk))
        turn = (-steps) % LANES if isinstance(steps, int) else jnp.where(steps > 0, LANES - steps, -steps)
        low = tall(lane < plan.side + steps, chunk)
        return pltpu.roll(jnp.where(low, window[1], window[0]), turn, 1)

    edge = jnp.zeros((PAD, LANES), jnp.float32)
    above, below = slice(0, PAD), slice(PAD + total, PAD + total + PAD)
    for t in tiles:
        keep[t, above, :] = edge
        keep[t, below, :] = edge
        for g in range(dirs):
            q[g, t, above, :] = edge
            q[g, t, below, :] = edge
            for i in range(2):
                phase[g, i, t, above, :] = edge
                phase[g, i, t, below, :] = edge
        for layer in range(layers):
            for ref in (v0, v1, smooth):
                ref[layer, t, above, :] = edge
                ref[layer, t, below, :] = edge
    sources = []
    if plan.direct:
        core = tile_place % 2
        for i, field in enumerate(fields):
            tile = 2 * ((tile_place // 2) ^ (i % plan.outs)) + (core if i < plan.outs else 1 - core)
            low = [(core + t) * plan.used_rows for t in tiles]
            sources.append((tile, [(field, start) for start in low]))
    else:
        for tile in range(plan.tiles):
            sources.append((tile, [(fields[0].at[tile, t], 0) for t in tiles]))
    for tile, windows in sources:
        here = pl.ds(PAD + tile * rows, rows)
        for t, (window, start) in enumerate(windows):
            keep[t, here, :] = window[pl.ds(start + dirs * rows, rows), :]
            for g in range(dirs):
                q[g, t, here, :] = window[pl.ds(start + g * rows, rows), :]
    for tile, windows in sources:
        below = pl.ds(PAD + (tile + 1) * rows, 1)
        counts = jnp.where(tile + 1 < plan.tiles, 1.0, 0.0)
        for t, (window, start) in enumerate(windows):
            for g in range(dirs):
                carry = start + (dirs + 1) * rows + g
                q[g, t, below, :] += window[pl.ds(carry, 1), :] * counts

    def four(x, up, down, left, right):
        return 4.0 * x - (up + down) - (left + right)

    def rows_at(r, by=0):
        return slice(PAD + r + by, PAD + r + by + chunk)

    def staged(first, second):
        for i, r in enumerate(starts):
            first(r)
            if i:
                second(starts[i - 1])
        second(starts[-1])

    def laplace(ref, layer, r, shift):
        x = [ref[layer, t, rows_at(r), :] for t in tiles]
        right = shift(x, 1)
        left = shift(x, -1)
        column = [
            4.0 * x[t] - (ref[layer, t, rows_at(r, -1), :] + ref[layer, t, rows_at(r, 1), :])
            for t in tiles
        ]
        if shift is packed_shift:
            return [pack(column) - (left + right)]
        return [column[t] - (left[t] + right[t]) for t in tiles]

    def window_shift(window, steps):
        return lane_shift(window, steps, chunk)

    def back_project(layer, level):
        source = (None, v0, v1)[level]
        shift = packed_shift if level == 2 else window_shift

        def smoothing(r):
            if source is not None:
                for t, value in enumerate(laplace(source, layer, r, window_shift)):
                    smooth[layer, t, rows_at(r), :] = value * in_grid[t]

        def adding(r):
            sums = None
            for g in range(dirs):
                low = PAD + r - offsets[layer, 0, g]
                window = [q[g, t, pl.ds(low, chunk), :] for t in tiles]
                moved = shift(window, -offsets[layer, 1, g])
                moved = [moved] if level == 2 else moved
                sums = moved if sums is None else [s + m for s, m in zip(sums, moved)]
            sums = [0.5 * value for value in sums]
            if source is not None:
                weight = weights[layer]
                sums = [s + weight * value for s, value in zip(sums, laplace(smooth, layer, r, shift))]
            if level == 2:
                packed[2, layer, r : r + chunk, :] = sums[0]
                return
            sums = [s * inside for s, inside in zip(sums, in_grid)]
            for t in tiles:
                (v0, v1)[level][layer, t, rows_at(r), :] = sums[t]
            packed[level, layer, r : r + chunk, :] = pack(sums)

        staged(smoothing, adding)

    def project(g, source):
        def phases(r):
            sums = None
            for layer in range(layers):
                low = PAD + r + offsets[layer, 0, g]
                window = [source[layer, t, pl.ds(low, chunk), :] for t in tiles]
                moved = lane_shift(window, offsets[layer, 1, g], chunk)
                sums = moved if sums is None else [s + m for s, m in zip(sums, moved)]
            sums = [s * inside for s, inside in zip(sums, in_grid)]
            right = lane_shift(sums, 1, chunk)
            for t in tiles:
                phase[g, 0, t, rows_at(r), :] = sums[t]
                phase[g, 1, t, rows_at(r), :] = right[t]

        def slopes(r):
            ahead, level = [], []
            for t in tiles:
                p00, p01 = phase[g, 0, t, rows_at(r), :], phase[g, 1, t, rows_at(r), :]
                p10, p11 = phase[g, 0, t, rows_at(r, 1), :], phase[g, 1, t, rows_at(r, 1), :]
                up0, up1 = phase[g, 0, t, rows_at(r, -1), :], phase[g, 1, t, rows_at(r, -1), :]
                mask, mask_up = keep[t, rows_at(r), :], keep[t, rows_at(r, -1), :]
                ahead.append(mask * (p01 - p10) + mask_up * (p01 - up0))
                level.append(mask * (p11 - p00) + mask_up * (up1 - p00))
            ahead = lane_shift(ahead, -1, chunk)
            for t in tiles:
                q[g, t, rows_at(r), :] = (ahead[t] - level[t]) * in_grid[t]

        staged(phases, slopes)

    def each(count, body):
        if unrolled:
            for i in range(count):
                body(i)
            return

        def step(i, carry):
            body(i)
            return carry

        lax.fori_loop(0, count, step, 0)

    def fold(value):
        return jnp.sum(value.reshape(chunk // 8, 8, LANES), axis=0)

    def inner(terms, layer, sums):
        for r in starts:
            values = terms([packed[i, layer, r : r + chunk, :] for i in range(3)])
            sums = [s + fold(value) for s, value in zip(sums, values)]
        return sums

    def send(i, layer):
        device, own = layer // plan.own_layers, layer % plan.own_layers
        for s in range(plan.tiles):
            block = packed[i, layer, s * rows : (s + 1) * rows, :]
            if plan.own < LANES:
                block = pltpu.roll(block, (-plan.side) % LANES, 1)[:, : plan.own]
            at = (own * 3 + i) * rows
            out[device * plan.tiles + s, at : at + rows, :] = block

    def first_terms(fields):
        a, b, _ = fields
        return a * a, a * b, b * b

    each(layers, lambda layer: back_project(layer, 0))
    each(dirs, lambda g: project(g, v0))
    each(layers, lambda layer: back_project(layer, 1))
    def second_terms(fields):
        a, b, c = fields
        e = a - spread * b
        f = b - spread * c
        return e * e, e * b, e * f, e * c + b * f, b * c

    sums = [jnp.zeros((8, LANES), jnp.float32)] * 3
    more = [jnp.zeros((8, LANES), jnp.float32)] * 5
    if not unrolled:
        each(dirs, lambda g: project(g, v1))
    for i in range(max(layers, dirs)):
        if unrolled and i < dirs:
            project(i, v1)
        if i < layers:
            sums = inner(first_terms, i, sums)
            send(0, i)
            send(1, i)
    s00, s01, s11 = [jnp.sum(value, keepdims=True) for value in sums]
    coefficient = jnp.where(s11 > 0.0, s01 / jnp.where(s11 > 0.0, s11, 1.0), 0.0)
    spread = jnp.broadcast_to(coefficient, (chunk, LANES))
    if not unrolled:
        each(layers, lambda layer: back_project(layer, 2))
    for layer in range(layers):
        if unrolled:
            back_project(layer, 2)
        more = inner(second_terms, layer, more)
        send(2, layer)
    more = [jnp.sum(value, keepdims=True) for value in more]
    scalars = [s00, s01, s11, coefficient] + more
    row = jnp.zeros((1, LANES), jnp.float32)
    for i, value in enumerate(scalars):
        row = jnp.where(lane[:1] == i, value, row)
    tail = 3 * plan.own_layers * rows
    note = jnp.broadcast_to(row[:, : plan.own], (plan.out_rows - tail, plan.own))
    for to in range(plan.devices):
        out[to, tail:, :] = note


def coefficients(notes):
    s00, s01, s11, c, ee, eb, ef, mixed, bc = [notes[:, i : i + 1] for i in range(9)]

    def total(value):
        return jnp.sum(value, axis=0, keepdims=True)

    norm_0 = total(s00)
    power_0 = total(s01)
    alpha_0 = norm_0 / power_0
    delta = alpha_0 - c
    norm_1 = total(ee - 2.0 * delta * eb + delta * delta * s11)
    beta = norm_1 / norm_0
    power_1 = (
        total(ef - delta * mixed + delta * delta * bc)
        + 2.0 * beta * total(eb - delta * s11)
        + beta * beta * power_0
    )
    return alpha_0, beta, norm_1 / power_1


def weights_of(scalars):
    alpha_0, beta, alpha_1 = scalars
    return alpha_0 + alpha_1 * (1.0 + beta), -alpha_1 * alpha_0


def combine_kernel(plan, blocks, estimate, residual, lines, sems):
    rows = plan.rows
    tail = 3 * plan.own_layers * rows
    near, far = [
        jnp.broadcast_to(value, (rows, LANES))
        for value in weights_of(coefficients(blocks[:, tail, :]))
    ]
    copies = [
        pltpu.make_async_copy(lines.at[i], ref, sems.at[i])
        for i, ref in enumerate((estimate, residual))
    ]
    for i, copy in enumerate(copies):
        for k in range(plan.devices):
            for own in range(plan.own_layers):
                field = [
                    blocks[k, (own * 3 + j) * rows : (own * 3 + j + 1) * rows, :]
                    for j in range(i, i + 2)
                ]
                value = near * field[0] + far * field[1]
                if i:
                    value = blocks[k, own * 3 * rows : (own * 3 + 1) * rows, :] - value
                where = pl.ds(own * rows * plan.devices + k, rows, stride=plan.devices)
                lines.at[i][where, :] = pltpu.roll(value, (-plan.side) % LANES, 1)
        copy.start()
    for copy in copies:
        copy.wait()


def combine(plan, blocks):
    shape = (plan.own_layers, plan.rows, plan.width)
    if plan.own == LANES:
        lines = (plan.own_layers * plan.rows * plan.devices, LANES)
        results = pl.pallas_call(
            functools.partial(combine_kernel, plan),
            out_shape=[jax.ShapeDtypeStruct(lines, jnp.float32)] * 2,
            in_specs=[pl.BlockSpec(memory_space=VMEM)],
            out_specs=[pl.BlockSpec(memory_space=pl.ANY)] * 2,
            scratch_shapes=[
                pltpu.VMEM((2,) + lines, jnp.float32),
                pltpu.SemaphoreType.DMA((2,)),
            ],
            name="combine",
        )(in_vmem(blocks))
        return [value.reshape(shape) for value in results]
    tail = 3 * plan.own_layers * plan.rows
    scalars = coefficients(blocks[:, tail, :])
    fields = blocks[:, :tail].reshape(plan.devices, plan.own_layers, 3, plan.rows, plan.own)
    fields = fields.transpose(2, 1, 3, 0, 4).reshape((3,) + shape)
    near, far = weights_of([value[0, 0] for value in scalars])
    a, b, c = fields
    return near * a + far * b, a - (near * b + far * c)


def per_device(mesh, measured_slopes, valid_mask, layer_offsets, reg_weight):
    dirs, _, rows, width = measured_slopes.shape
    plan = Plan(mesh, dirs, rows, width, reg_weight.shape[0])
    column_tiles = width // LANES
    slopes = measured_slopes.reshape(dirs, 2, rows, column_tiles, LANES)
    slopes = slopes.transpose(0, 2, 3, 1, 4).reshape(dirs, rows, 2 * column_tiles, LANES)
    strips = plan.strip // LANES
    piece = (plan.tiles, plan.sent_tiles, plan.in_rows, LANES)
    if plan.direct:
        piece = (round_up(plan.sent_tiles * plan.used_rows, 8), LANES)
    kind = pltpu.VMEM if plan.direct else jax.ShapeDtypeStruct
    sent = pl.pallas_call(
        functools.partial(gather_kernel, plan),
        out_shape=[kind(piece, jnp.float32)] * plan.outs,
        in_specs=[pl.BlockSpec(memory_space=pl.ANY)] * 2,
        out_specs=[pl.BlockSpec(memory_space=VMEM)] * plan.outs,
        scratch_shapes=[
            pltpu.VMEM((dirs, plan.high, plan.raw_rows, LANES), jnp.float32),
            pltpu.VMEM((rows, plan.strip), jnp.int32),
            pltpu.VMEM((strips, plan.in_rows, LANES), jnp.float32),
            pltpu.VMEM((strips - 1, plan.in_rows, LANES), jnp.float32),
            pltpu.SemaphoreType.DMA((dirs + 1,)),
        ],
        name="gather",
    )(slopes, valid_mask)
    if plan.direct:
        fields = list(sent)
        for k in reversed(range(1, plan.outs)):
            fields[k] = lax.ppermute(sent[k], "tile", [(i, i ^ (2 * k)) for i in range(plan.tiles)])
        swap = [(i, i ^ 1) for i in range(plan.tiles)]
        fields = fields + [lax.ppermute(field, "tile", swap) for field in fields]
    else:
        fields = [lax.all_to_all(sent[0], "tile", 0, 0)]
    fields = [in_vmem(field) for field in fields]
    tall_rows = plan.grid_rows + 2 * PAD

    def scratch(*lead):
        return pltpu.VMEM(lead + (plan.lane_tiles, tall_rows, LANES), jnp.float32)

    blocks = pl.pallas_call(
        functools.partial(solve_kernel, plan),
        out_shape=kind((plan.devices, plan.out_rows, plan.own), jnp.float32),
        in_specs=[pl.BlockSpec(memory_space=SMEM)] * 2
        + [pl.BlockSpec(memory_space=VMEM)] * len(fields),
        out_specs=pl.BlockSpec(memory_space=VMEM),
        scratch_shapes=[
            scratch(dirs),
            scratch(),
            scratch(plan.layers),
            scratch(plan.layers),
            scratch(dirs, 2),
            scratch(plan.layers),
            pltpu.VMEM((3, plan.layers, plan.grid_rows, LANES), jnp.float32),
        ],
        name="solve",
    )(layer_offsets.transpose(1, 2, 0), reg_weight, *fields)
    blocks = lax.all_to_all(blocks, ("layer", "tile"), 0, 0)
    return tuple(combine(plan, blocks))


def solution(mesh):
    return jax.shard_map(
        functools.partial(per_device, mesh),
        mesh=mesh,
        in_specs=(P(None, None, "tile", None), P("tile", None), P(), P()),
        out_specs=(P("layer", "tile", None), P("layer", "tile", None)),
        check_vma=False,
    )
```

time: 47.9 us -> 46.6 us (0.973)
  Pallas kernels: 11.2 us -> 10.3 us
where the time goes in v4:
time: 46.6 us; the launch traced here: 46.4 us
  blocking collectives  22.7 us (49%)
  Pallas kernels  10.3 us (22%)
  waiting for transfers between devices  7.61 us (16%)
  starting transfers between devices  5.09 us (11%)
  between operations  0.65 us (1%)
    all_to_all x1, blocking collectives, per_device(): blocks = lax.all_to_all(blocks, ('layer', 'tile'), 0, 0)  22.7 us
    pallas_call x1, Pallas kernels, per_device(): pl.pallas_call(functools.partial(solve_kernel, plan), out_shape=kind((pla...  7.14 us
    ppermute x3, waiting for transfers between devices, per_device(): lax.ppermute(sent[k], 'tile', [(i, i ^ 2 * k) for i in range(plan.tiles)])  6.57 us
    ppermute x3, starting transfers between devices, per_device(): lax.ppermute(sent[k], 'tile', [(i, i ^ 2 * k) for i in range(plan.tiles)])  4.57 us
    pallas_call x1, Pallas kernels, per_device(): pl.pallas_call(functools.partial(gather_kernel, plan), out_shape=[kind(pi...  1.94 us
    pallas_call x1, Pallas kernels, combine(): pl.pallas_call(functools.partial(combine_kernel, plan), out_shape=[jax.Sh...  1.23 us
    ppermute x4, waiting for transfers between devices, per_device(): fields = fields + [lax.ppermute(field, 'tile', swap) for field in fields]  1.04 us
  transfers between devices with their start and end apart: 7, of which 4 were waited for; matrix products, arithmetic and copies ran while one was open for 0% of the time, Pallas kernels for 0%

profile of v4, /device:TPU:0, one launch (start us, length us, event | category | flops | bytes accessed | tf_op | source)
XLA Modules:
  0.0 46.4 jit_solution(17474166812638118101)
XLA Ops:
  0.6 1.9 %gather.1 = (f32[272,128]{1,0:T(8,128)S(1)}, f32[272,128]{1,0:T(8,128)S(1)}, f32[272,128]{1,0:T(8,128)S(1)}, f32[272,128]{1,0:T(8,128)S(1)}) custom-call(f32[6,12,64,128]{3,2,1,0:T(8,128)} %bitcast.8, s32[12,4096]{1,0:T(8,128)} %mask.1), custom_call_target="tpu_custom_call" | custom-call | tf_op jit(solution)/shard_map/gather/pallas_call | solution.py:515
  2.6 3.0 %collective-permute-start = (f32[272,128]{1,0:T(8,128)S(1)}, f32[272,128]{1,0:T(8,128)S(1)}, u32[]{:S(2)}, u32[]{:S(2)}) collective-permute-start(f32[272,128]{1,0:T(8,128)S(1)} %get-tuple-element.9), channel_id=1, source_target_pairs={{0,2},{1,3},{2,0},{3,1},{4,6},{5,7},{6,4},{7,5},{8,10},{9,11},{10,... | collective-permute-start | bytes 417800 | tf_op jit(solution)/shard_map/ppermute | solution.py:532
  5.6 1.5 %collective-permute-start.1 = (f32[272,128]{1,0:T(8,128)S(1)}, f32[272,128]{1,0:T(8,128)S(1)}, u32[]{:S(2)}, u32[]{:S(2)}) collective-permute-start(f32[272,128]{1,0:T(8,128)S(1)} %get-tuple-element.10), channel_id=1, source_target_pairs={{0,4},{1,5},{2,6},{3,7},{4,0},{5,1},{6,2},{7,3},{8,12},{9,13},{10,... | collective-permute-start | bytes 417800 | tf_op jit(solution)/shard_map/ppermute | solution.py:532
  7.1 0.0 collective-permute-start.2
  7.2 0.0 collective-permute-start.3
  7.2 2.5 %collective-permute-done.refs_1_ = f32[272,128]{1,0:T(8,128)S(1)} collective-permute-done((f32[272,128]{1,0:T(8,128)S(1)}, f32[272,128]{1,0:T(8,128)S(1)}, u32[]{:S(2)}, u32[]{:S(2)}) %collective-permute-start) | collective-permute-done | bytes 139296 | tf_op jit(solution)/shard_map/ppermute | solution.py:532
  9.7 0.0 collective-permute-start.4
  9.7 4.1 %collective-permute-done.1.refs_2_ = f32[272,128]{1,0:T(8,128)S(1)} collective-permute-done((f32[272,128]{1,0:T(8,128)S(1)}, f32[272,128]{1,0:T(8,128)S(1)}, u32[]{:S(2)}, u32[]{:S(2)}) %collective-permute-start.1) | collective-permute-done | bytes 139296 | tf_op jit(solution)/shard_map/ppermute | solution.py:532
  13.7 0.0 collective-permute-start.5
  13.7 0.0 collective-permute-done.2.refs_3_
  13.7 0.5 %collective-permute-start.6 = (f32[272,128]{1,0:T(8,128)S(1)}, f32[272,128]{1,0:T(8,128)S(1)}, u32[]{:S(2)}, u32[]{:S(2)}) collective-permute-start(f32[272,128]{1,0:T(8,128)S(1)} %collective-permute-done.2.refs_3_), channel_id=1, source_target_pairs={{0,1},{1,0},{2,3},{3,2},{4,5},{5,4},{6,7},{7,6},{8,9},{9,8},{10,11... | collective-permute-start | bytes 417800 | tf_op jit(solution)/shard_map/ppermute | solution.py:534
  14.2 0.0 collective-permute-done.3.refs_4_
  14.2 0.0 collective-permute-done.4.refs_5_
  14.3 0.8 %collective-permute-done.5.refs_6_ = f32[272,128]{1,0:T(8,128)S(1)} collective-permute-done((f32[272,128]{1,0:T(8,128)S(1)}, f32[272,128]{1,0:T(8,128)S(1)}, u32[]{:S(2)}, u32[]{:S(2)}) %collective-permute-start.5) | collective-permute-done | bytes 139296 | tf_op jit(solution)/shard_map/ppermute | solution.py:534
  15.1 0.2 collective-permute-done.6.refs_7_
  15.3 7.1 %solve.1 = f32[32,40,128]{2,1,0:T(8,128)S(1)} custom-call(s32[4,2,6]{2,1,0:T(2,128)} %bitcast.9, f32[4]{0:T(128)} %weights.1, f32[272,128]{1,0:T(8,128)S(1)} %get-tuple-element.8.refs_0_, f32[272,128]{1,0:T(8,128)S(1)} %collective-permute-done.refs_1_, f32[272,128]{1,0:T(8,128)S(1)} %collective-permute-done.1.refs_2_, ...), custom_call_target="tpu_custom_call" | custom-call | tf_op jit(solution)/shard_map/solve/pallas_call | solution.py:543
  22.4 22.7 %all_to_all.5.blocks = f32[32,40,128]{2,1,0:T(8,128)S(1)} all-to-all(f32[32,40,128]{2,1,0:T(8,128)S(1)} %solve.1), channel_id=1, replica_groups=mesh['layer'=4,'tile'=8] {'layer','tile'}, dimensions={0} | all-to-all | bytes 1310720 | tf_op jit(solution)/shard_map/all_to_all | solution.py:560
  45.2 1.2 %combine.1 = (f32[384,128]{1,0:T(8,128)}, f32[384,128]{1,0:T(8,128)}) custom-call(f32[32,40,128]{2,1,0:T(8,128)S(1)} %all_to_all.5.blocks), custom_call_target="tpu_custom_call" | custom-call | tf_op jit(solution)/shard_map/combine/pallas_call | solution.py:483
Async XLA Ops:
  2.6 7.1 %collective-permute-start = (f32[272,128]{1,0:T(8,128)S(1)}, f32[272,128]{1,0:T(8,128)S(1)}, u32[]{:S(2)}, u32[]{:S(2)}) collective-permute-start(f32[272,128]{1,0:T(8,128)S(1)} %get-tuple-element.9), channel_id=1, source_target_pairs={{0,2},{1,3},{2,0},{3,1},{4,6},{5,7},{6,4},{7,5},{8,10},{9,11},{10,... | collective-permute-start | bytes 417800 | tf_op jit(solution)/shard_map/ppermute | solution.py:532
  5.6 8.1 %collective-permute-start.1 = (f32[272,128]{1,0:T(8,128)S(1)}, f32[272,128]{1,0:T(8,128)S(1)}, u32[]{:S(2)}, u32[]{:S(2)}) collective-permute-start(f32[272,128]{1,0:T(8,128)S(1)} %get-tuple-element.10), channel_id=1, source_target_pairs={{0,4},{1,5},{2,6},{3,7},{4,0},{5,1},{6,2},{7,3},{8,12},{9,13},{10,... | collective-permute-start | bytes 417800 | tf_op jit(solution)/shard_map/ppermute | solution.py:532
  7.1 6.6 %collective-permute-start.2 = (f32[272,128]{1,0:T(8,128)S(1)}, f32[272,128]{1,0:T(8,128)S(1)}, u32[]{:S(2)}, u32[]{:S(2)}) collective-permute-start(f32[272,128]{1,0:T(8,128)S(1)} %get-tuple-element.11), channel_id=1, source_target_pairs={{0,6},{1,7},{2,4},{3,5},{4,2},{5,3},{6,0},{7,1},{8,14},{9,15},{10,... | collective-permute-start | bytes 417800 | tf_op jit(solution)/shard_map/ppermute | solution.py:532
  7.2 7.1 %collective-permute-start.3 = (f32[272,128]{1,0:T(8,128)S(1)}, f32[272,128]{1,0:T(8,128)S(1)}, u32[]{:S(2)}, u32[]{:S(2)}) collective-permute-start(f32[272,128]{1,0:T(8,128)S(1)} %get-tuple-element.8.refs_0_), channel_id=1, source_target_pairs={{0,1},{1,0},{2,3},{3,2},{4,5},{5,4},{6,7},{7,6},{8,9},{9,8},{10,11... | collective-permute-start | bytes 417800 | tf_op jit(solution)/shard_map/ppermute | solution.py:534
  9.7 4.6 %collective-permute-start.4 = (f32[272,128]{1,0:T(8,128)S(1)}, f32[272,128]{1,0:T(8,128)S(1)}, u32[]{:S(2)}, u32[]{:S(2)}) collective-permute-start(f32[272,128]{1,0:T(8,128)S(1)} %collective-permute-done.refs_1_), channel_id=1, source_target_pairs={{0,1},{1,0},{2,3},{3,2},{4,5},{5,4},{6,7},{7,6},{8,9},{9,8},{10,11... | collective-permute-start | bytes 417800 | tf_op jit(solution)/shard_map/ppermute | solution.py:534
  13.7 1.4 %collective-permute-start.5 = (f32[272,128]{1,0:T(8,128)S(1)}, f32[272,128]{1,0:T(8,128)S(1)}, u32[]{:S(2)}, u32[]{:S(2)}) collective-permute-start(f32[272,128]{1,0:T(8,128)S(1)} %collective-permute-done.1.refs_2_), channel_id=1, source_target_pairs={{0,1},{1,0},{2,3},{3,2},{4,5},{5,4},{6,7},{7,6},{8,9},{9,8},{10,11... | collective-permute-start | bytes 417800 | tf_op jit(solution)/shard_map/ppermute | solution.py:534
  13.7 1.6 %collective-permute-start.6 = (f32[272,128]{1,0:T(8,128)S(1)}, f32[272,128]{1,0:T(8,128)S(1)}, u32[]{:S(2)}, u32[]{:S(2)}) collective-permute-start(f32[272,128]{1,0:T(8,128)S(1)} %collective-permute-done.2.refs_3_), channel_id=1, source_target_pairs={{0,1},{1,0},{2,3},{3,2},{4,5},{5,4},{6,7},{7,6},{8,9},{9,8},{10,11... | collective-permute-start | bytes 417800 | tf_op jit(solution)/shard_map/ppermute | solution.py:534

commit v5 on v4

--- a/solution.py
+++ b/solution.py
@@ -38,11 +38,6 @@
         self.lane_tiles = round_up(self.own + 2 * REACH, LANES) // LANES
         self.side = (self.lane_tiles * LANES - self.own) // 2
         self.margin = round_up(self.side + 1, LANES)
-        self.strip = self.part + 2 * self.margin
-        assert self.margin <= 4 * LANES and (2 * self.part // LANES) % 8 == 0
-        self.raw_core = min(2 * self.part // LANES + 16, 2 * width // LANES)
-        self.raw_rows = 2 * self.part // LANES + 32
-        assert self.strip <= width
         self.high = round_up(rows + 1, 8)
         self.used_rows = dirs * (rows + 1) + rows
         self.in_rows = round_up(self.used_rows, 8)
@@ -50,6 +45,15 @@
         self.chips = self.tiles // 2
         self.direct = self.tiles in (2, 4, 8) and self.own == LANES and self.lane_tiles == 2
         self.outs = self.chips if self.direct else 1
+        self.halves = 1
+        if self.direct and self.chips == 4 and self.part % (8 * LANES) == 0:
+            self.halves = 2
+        self.stretch = self.part // self.halves
+        self.strip = self.stretch + 2 * self.margin
+        assert self.margin <= 4 * LANES and (2 * self.stretch // LANES) % 8 == 0
+        self.raw_core = min(2 * self.stretch // LANES + 16, 2 * width // LANES)
+        self.raw_rows = 2 * self.stretch // LANES + 32
+        assert self.strip <= width
         self.sent_tiles = self.lane_tiles + 1 if self.direct else self.lane_tiles
         self.chunk = self.grid_rows
         while self.chunk > (96 if self.direct else 192):
@@ -97,13 +101,17 @@
     return lax.axis_index("layer"), lax.axis_index("tile")
 
 
-def gather_kernel(plan, slopes, mask, *refs):
-    outs, (raw, raw_mask, strip, ready, sems) = refs[: plan.outs], refs[plan.outs :]
+def gather_kernel(plan, slots, slopes, mask, *refs):
+    count = len(slots) if plan.direct else 1
+    outs, (raw, raw_mask, strip, ready, sems) = refs[-5 - count : -5], refs[-5:]
     layer, tile = place_of()
-    rows, dirs, part, width = plan.rows, plan.dirs, plan.part, plan.width
+    rows, dirs, width = plan.rows, plan.dirs, plan.width
     side = plan.margin
-    column = layer * part - side
-    line = 2 * (layer * part // LANES)
+    stretch = layer * plan.halves
+    if plan.halves == 2:
+        stretch = stretch + (((tile // 2) ^ slots[0]) // 2)
+    column = stretch * plan.stretch - side
+    line = stretch * (2 * plan.stretch // LANES)
     base = jnp.clip(column, 0, width - plan.strip)
     base_line = jnp.clip(line - 8, 0, 2 * width // LANES - plan.raw_core)
     slope_copies = [
@@ -171,10 +179,11 @@
 
     begin = plan.margin - plan.side
     if plan.direct:
-        for n in range(2 * plan.chips + 1):
+        near = plan.chips // plan.halves
+        for n in range(2 * near + 1):
             ready[n] = turn(begin // LANES + n, begin % LANES)
-        for k, out in enumerate(outs):
-            at = 2 * ((tile // 2) ^ k)
+        for k, out in zip(slots, outs):
+            at = 2 * (((tile // 2) ^ k) % near)
             for n in range(plan.sent_tiles):
                 out[plan.used_rows * n : plan.used_rows * (n + 1), :] = ready[
                     at + n, : plan.used_rows, :
@@ -512,20 +521,31 @@
     if plan.direct:
         piece = (round_up(plan.sent_tiles * plan.used_rows, 8), LANES)
     kind = pltpu.VMEM if plan.direct else jax.ShapeDtypeStruct
-    sent = pl.pallas_call(
-        functools.partial(gather_kernel, plan),
-        out_shape=[kind(piece, jnp.float32)] * plan.outs,
-        in_specs=[pl.BlockSpec(memory_space=pl.ANY)] * 2,
-        out_specs=[pl.BlockSpec(memory_space=VMEM)] * plan.outs,
-        scratch_shapes=[
-            pltpu.VMEM((dirs, plan.high, plan.raw_rows, LANES), jnp.float32),
-            pltpu.VMEM((rows, plan.strip), jnp.int32),
-            pltpu.VMEM((strips, plan.in_rows, LANES), jnp.float32),
-            pltpu.VMEM((strips - 1, plan.in_rows, LANES), jnp.float32),
-            pltpu.SemaphoreType.DMA((dirs + 1,)),
-        ],
-        name="gather",
-    )(slopes, valid_mask)
+
+    def gather(slots, after):
+        return pl.pallas_call(
+            functools.partial(gather_kernel, plan, slots),
+            out_shape=[kind(piece, jnp.float32)] * len(slots),
+            in_specs=[pl.BlockSpec(memory_space=pl.ANY)] * (2 + len(after)),
+            out_specs=[pl.BlockSpec(memory_space=VMEM)] * len(slots),
+            scratch_shapes=[
+                pltpu.VMEM((dirs, plan.high, plan.raw_rows, LANES), jnp.float32),
+                pltpu.VMEM((rows, plan.strip), jnp.int32),
+                pltpu.VMEM((strips, plan.in_rows, LANES), jnp.float32),
+                pltpu.VMEM((strips - 1, plan.in_rows, LANES), jnp.float32),
+                pltpu.SemaphoreType.DMA((dirs + 1,)),
+            ],
+            cost_estimate=pl.CostEstimate(
+                flops=10_000_000, bytes_accessed=2_000_000, transcendentals=0
+            ),
+            name="gather",
+        )(slopes, valid_mask, *after)
+
+    if plan.halves == 2:
+        far = gather((2, 3), ())
+        sent = gather((0, 1), far[:1]) + far
+    else:
+        sent = gather(tuple(range(plan.outs)), ())
     if plan.direct:
         fields = list(sent)
         for k in reversed(range(1, plan.outs)):

time: 46.6 us -> 46.3 us (level)
  Pallas kernels: 10.3 us -> 11.8 us
  waiting for transfers between devices: 7.61 us -> 6.24 us
    ppermute x3, waiting for transfers between devices: 6.57 us -> 4.89 us  [per_device(): lax.ppermute(sent[k], 'tile', [(i, i ^ 2 * k) for i in range(plan.tiles)])]
    pallas_call x1 -> x2, Pallas kernels: 1.94 us -> 3.41 us  [gather(): pl.pallas_call(functools.partial(gather_kernel, plan, slots), out_shape=[...]
    ppermute x4, starting transfers between devices: 0.52 us -> 0.02 us  [per_device(): fields = fields + [lax.ppermute(field, 'tile', swap) for field in fields]]
  transfers between devices with their start and end apart: 7 -> 7, of which waited for: 4 -> 5; matrix products, arithmetic and copies ran while one was open for 0% -> 0% of each run, Pallas kernels for 0% -> 4%
where the time goes in v5:
time: 46.3 us; the launch traced here: 46.1 us
  blocking collectives  22.7 us (49%)
  Pallas kernels  11.8 us (25%)
  waiting for transfers between devices  6.24 us (13%)
  starting transfers between devices  4.73 us (10%)
  between operations  0.67 us (1%)
    all_to_all x1, blocking collectives, per_device(): blocks = lax.all_to_all(blocks, ('layer', 'tile'), 0, 0)  22.7 us
    pallas_call x1, Pallas kernels, per_device(): pl.pallas_call(functools.partial(solve_kernel, plan), out_shape=kind((pla...  7.14 us
    ppermute x3, waiting for transfers between devices, per_device(): lax.ppermute(sent[k], 'tile', [(i, i ^ 2 * k) for i in range(plan.tiles)])  4.89 us
    ppermute x3, starting transfers between devices, per_device(): lax.ppermute(sent[k], 'tile', [(i, i ^ 2 * k) for i in range(plan.tiles)])  4.7 us
    pallas_call x2, Pallas kernels, gather(): pl.pallas_call(functools.partial(gather_kernel, plan, slots), out_shape=[...  3.41 us
    ppermute x4, waiting for transfers between devices, per_device(): fields = fields + [lax.ppermute(field, 'tile', swap) for field in fields]  1.35 us
    pallas_call x1, Pallas kernels, combine(): pl.pallas_call(functools.partial(combine_kernel, plan), out_shape=[jax.Sh...  1.23 us
  transfers between devices with their start and end apart: 7, of which 5 were waited for; matrix products, arithmetic and copies ran while one was open for 0% of the time, Pallas kernels for 4%

profile of v5, /device:TPU:0, one launch (start us, length us, event | category | flops | bytes accessed | tf_op | source)
XLA Modules:
  0.0 46.1 jit_solution(1585295796020994720)
XLA Ops:
  0.6 1.7 %gather.2 = (f32[272,128]{1,0:T(8,128)S(1)}, f32[272,128]{1,0:T(8,128)S(1)}) custom-call(f32[6,12,64,128]{3,2,1,0:T(8,128)} %bitcast.8, s32[12,4096]{1,0:T(8,128)} %mask.3), custom_call_target="tpu_custom_call" | custom-call | flops 10000000 | bytes 2000000 | tf_op jit(solution)/shard_map/gather/pallas_call | solution.py:526
  2.4 0.0 copy-start
  2.4 4.0 %collective-permute-start.2 = (f32[272,128]{1,0:T(8,128)S(1)}, f32[272,128]{1,0:T(8,128)S(1)}, u32[]{:S(2)}, u32[]{:S(2)}) collective-permute-start(f32[272,128]{1,0:T(8,128)S(1)} %get-tuple-element.11), channel_id=1, source_target_pairs={{0,6},{1,7},{2,4},{3,5},{4,2},{5,3},{6,0},{7,1},{8,14},{9,15},{10,... | collective-permute-start | bytes 417800 | tf_op jit(solution)/shard_map/ppermute | solution.py:552
  6.4 0.5 %collective-permute-start.1 = (f32[272,128]{1,0:T(8,128)S(1)}, f32[272,128]{1,0:T(8,128)S(1)}, u32[]{:S(2)}, u32[]{:S(2)}) collective-permute-start(f32[272,128]{1,0:T(8,128)S(1)} %get-tuple-element.8.refs_0_), channel_id=1, source_target_pairs={{0,4},{1,5},{2,6},{3,7},{4,0},{5,1},{6,2},{7,3},{8,12},{9,13},{10,... | collective-permute-start | bytes 417800 | tf_op jit(solution)/shard_map/ppermute | solution.py:552
  6.9 0.0 copy-done
  6.9 1.7 %gather.3 = (f32[272,128]{1,0:T(8,128)S(1)}, f32[272,128]{1,0:T(8,128)S(1)}) custom-call(f32[6,12,64,128]{3,2,1,0:T(8,128)} %bitcast.9, s32[12,4096]{1,0:T(8,128)} %mask.3, f32[272,128]{1,0:T(8,128)} %copy-done), custom_call_target="tpu_custom_call" | custom-call | flops 10000000 | bytes 2000000 | tf_op jit(solution)/shard_map/gather/pallas_call | solution.py:526
  8.6 0.2 collective-permute-start
  8.8 0.0 collective-permute-start.3
  8.8 1.5 %collective-permute-done.2.refs_3_ = f32[272,128]{1,0:T(8,128)S(1)} collective-permute-done((f32[272,128]{1,0:T(8,128)S(1)}, f32[272,128]{1,0:T(8,128)S(1)}, u32[]{:S(2)}, u32[]{:S(2)}) %collective-permute-start.2) | collective-permute-done | bytes 139296 | tf_op jit(solution)/shard_map/ppermute | solution.py:552
  10.2 0.0 collective-permute-start.6
  10.2 2.8 %collective-permute-done.1.refs_2_ = f32[272,128]{1,0:T(8,128)S(1)} collective-permute-done((f32[272,128]{1,0:T(8,128)S(1)}, f32[272,128]{1,0:T(8,128)S(1)}, u32[]{:S(2)}, u32[]{:S(2)}) %collective-permute-start.1) | collective-permute-done | bytes 139296 | tf_op jit(solution)/shard_map/ppermute | solution.py:552
  13.0 0.0 collective-permute-start.5
  13.0 0.7 %collective-permute-done.refs_1_ = f32[272,128]{1,0:T(8,128)S(1)} collective-permute-done((f32[272,128]{1,0:T(8,128)S(1)}, f32[272,128]{1,0:T(8,128)S(1)}, u32[]{:S(2)}, u32[]{:S(2)}) %collective-permute-start) | collective-permute-done | bytes 139296 | tf_op jit(solution)/shard_map/ppermute | solution.py:552
  13.7 0.0 collective-permute-start.4
  13.7 0.0 collective-permute-done.3.refs_4_
  13.7 0.0 collective-permute-done.6.refs_7_
  13.7 0.7 %collective-permute-done.5.refs_6_ = f32[272,128]{1,0:T(8,128)S(1)} collective-permute-done((f32[272,128]{1,0:T(8,128)S(1)}, f32[272,128]{1,0:T(8,128)S(1)}, u32[]{:S(2)}, u32[]{:S(2)}) %collective-permute-start.5) | collective-permute-done | bytes 139296 | tf_op jit(solution)/shard_map/ppermute | solution.py:554
  14.4 0.7 %collective-permute-done.4.refs_5_ = f32[272,128]{1,0:T(8,128)S(1)} collective-permute-done((f32[272,128]{1,0:T(8,128)S(1)}, f32[272,128]{1,0:T(8,128)S(1)}, u32[]{:S(2)}, u32[]{:S(2)}) %collective-permute-start.4) | collective-permute-done | bytes 139296 | tf_op jit(solution)/shard_map/ppermute | solution.py:554
  15.0 7.1 %solve.1 = f32[32,40,128]{2,1,0:T(8,128)S(1)} custom-call(s32[4,2,6]{2,1,0:T(2,128)} %bitcast.10, f32[4]{0:T(128)} %weights.1, f32[272,128]{1,0:T(8,128)S(1)} %get-tuple-element.9.refs_0_, f32[272,128]{1,0:T(8,128)S(1)} %collective-permute-done.refs_1_, f32[272,128]{1,0:T(8,128)S(1)} %collective-permute-done.1.refs_2_, ...), custom_call_target="tpu_custom_call" | custom-call | tf_op jit(solution)/shard_map/solve/pallas_call | solution.py:563
  22.2 22.7 %all_to_all.5.blocks = f32[32,40,128]{2,1,0:T(8,128)S(1)} all-to-all(f32[32,40,128]{2,1,0:T(8,128)S(1)} %solve.1), channel_id=1, replica_groups=mesh['layer'=4,'tile'=8] {'layer','tile'}, dimensions={0} | all-to-all | bytes 1310720 | tf_op jit(solution)/shard_map/all_to_all | solution.py:580
  44.9 1.2 %combine.1 = (f32[384,128]{1,0:T(8,128)}, f32[384,128]{1,0:T(8,128)}) custom-call(f32[32,40,128]{2,1,0:T(8,128)S(1)} %all_to_all.5.blocks), custom_call_target="tpu_custom_call" | custom-call | tf_op jit(solution)/shard_map/combine/pallas_call | solution.py:492
Async XLA Ops:
  2.4 4.5 %copy-start = (f32[272,128]{1,0:T(8,128)}, f32[272,128]{1,0:T(8,128)S(1)}, u32[]{:S(2)}) copy-start(f32[272,128]{1,0:T(8,128)S(1)} %get-tuple-element.8.refs_0_) | copy-start | bytes 417796
  2.4 7.9 %collective-permute-start.2 = (f32[272,128]{1,0:T(8,128)S(1)}, f32[272,128]{1,0:T(8,128)S(1)}, u32[]{:S(2)}, u32[]{:S(2)}) collective-permute-start(f32[272,128]{1,0:T(8,128)S(1)} %get-tuple-element.11), channel_id=1, source_target_pairs={{0,6},{1,7},{2,4},{3,5},{4,2},{5,3},{6,0},{7,1},{8,14},{9,15},{10,... | collective-permute-start | bytes 417800 | tf_op jit(solution)/shard_map/ppermute | solution.py:552
  6.4 6.7 %collective-permute-start.1 = (f32[272,128]{1,0:T(8,128)S(1)}, f32[272,128]{1,0:T(8,128)S(1)}, u32[]{:S(2)}, u32[]{:S(2)}) collective-permute-start(f32[272,128]{1,0:T(8,128)S(1)} %get-tuple-element.8.refs_0_), channel_id=1, source_target_pairs={{0,4},{1,5},{2,6},{3,7},{4,0},{5,1},{6,2},{7,3},{8,12},{9,13},{10,... | collective-permute-start | bytes 417800 | tf_op jit(solution)/shard_map/ppermute | solution.py:552
  8.6 5.1 %collective-permute-start = (f32[272,128]{1,0:T(8,128)S(1)}, f32[272,128]{1,0:T(8,128)S(1)}, u32[]{:S(2)}, u32[]{:S(2)}) collective-permute-start(f32[272,128]{1,0:T(8,128)S(1)} %get-tuple-element.10), channel_id=1, source_target_pairs={{0,2},{1,3},{2,0},{3,1},{4,6},{5,7},{6,4},{7,5},{8,10},{9,11},{10,... | collective-permute-start | bytes 417800 | tf_op jit(solution)/shard_map/ppermute | solution.py:552
  8.8 4.9 %collective-permute-start.3 = (f32[272,128]{1,0:T(8,128)S(1)}, f32[272,128]{1,0:T(8,128)S(1)}, u32[]{:S(2)}, u32[]{:S(2)}) collective-permute-start(f32[272,128]{1,0:T(8,128)S(1)} %get-tuple-element.9.refs_0_), channel_id=1, source_target_pairs={{0,1},{1,0},{2,3},{3,2},{4,5},{5,4},{6,7},{7,6},{8,9},{9,8},{10,11... | collective-permute-start | bytes 417800 | tf_op jit(solution)/shard_map/ppermute | solution.py:554
  10.2 3.5 %collective-permute-start.6 = (f32[272,128]{1,0:T(8,128)S(1)}, f32[272,128]{1,0:T(8,128)S(1)}, u32[]{:S(2)}, u32[]{:S(2)}) collective-permute-start(f32[272,128]{1,0:T(8,128)S(1)} %collective-permute-done.2.refs_3_), channel_id=1, source_target_pairs={{0,1},{1,0},{2,3},{3,2},{4,5},{5,4},{6,7},{7,6},{8,9},{9,8},{10,11... | collective-permute-start | bytes 417800 | tf_op jit(solution)/shard_map/ppermute | solution.py:554
  13.0 1.4 %collective-permute-start.5 = (f32[272,128]{1,0:T(8,128)S(1)}, f32[272,128]{1,0:T(8,128)S(1)}, u32[]{:S(2)}, u32[]{:S(2)}) collective-permute-start(f32[272,128]{1,0:T(8,128)S(1)} %collective-permute-done.1.refs_2_), channel_id=1, source_target_pairs={{0,1},{1,0},{2,3},{3,2},{4,5},{5,4},{6,7},{7,6},{8,9},{9,8},{10,11... | collective-permute-start | bytes 417800 | tf_op jit(solution)/shard_map/ppermute | solution.py:554
  13.7 1.4 %collective-permute-start.4 = (f32[272,128]{1,0:T(8,128)S(1)}, f32[272,128]{1,0:T(8,128)S(1)}, u32[]{:S(2)}, u32[]{:S(2)}) collective-permute-start(f32[272,128]{1,0:T(8,128)S(1)} %collective-permute-done.refs_1_), channel_id=1, source_target_pairs={{0,1},{1,0},{2,3},{3,2},{4,5},{5,4},{6,7},{7,6},{8,9},{9,8},{10,11... | collective-permute-start | bytes 417800 | tf_op jit(solution)/shard_map/ppermute | solution.py:554

commit v6 on v5

--- a/solution.py
+++ b/solution.py
@@ -195,9 +195,18 @@
             outs[0][t, n] = turn(at // LANES + n, at % LANES)
 
 
-def solve_kernel(plan, offsets, weights, *refs):
+def solve_kernel(plan, all_offsets, all_weights, *refs):
     count = 2 * plan.outs if plan.direct else 1
-    fields, (out, q, keep, v0, v1, phase, smooth, packed) = refs[:count], refs[count:]
+    fields, (out, q, keep, v0, v1, phase, smooth, packed, offsets, weights, sems) = (
+        refs[:count],
+        refs[count:],
+    )
+    scalars_in = [
+        pltpu.make_async_copy(all_offsets, offsets, sems.at[0]),
+        pltpu.make_async_copy(all_weights, weights, sems.at[1]),
+    ]
+    for copy in scalars_in:
+        copy.start()
     layers, dirs, rows = plan.layers, plan.dirs, plan.rows
     total, tiles = plan.grid_rows, range(plan.lane_tiles)
     chunk = plan.chunk
@@ -391,6 +400,8 @@
         a, b, _ = fields
         return a * a, a * b, b * b
 
+    for copy in scalars_in:
+        copy.wait()
     each(layers, lambda layer: back_project(layer, 0))
     each(dirs, lambda g: project(g, v0))
     each(layers, lambda layer: back_project(layer, 1))
@@ -563,7 +574,7 @@
     blocks = pl.pallas_call(
         functools.partial(solve_kernel, plan),
         out_shape=kind((plan.devices, plan.out_rows, plan.own), jnp.float32),
-        in_specs=[pl.BlockSpec(memory_space=SMEM)] * 2
+        in_specs=[pl.BlockSpec(memory_space=pl.ANY)] * 2
         + [pl.BlockSpec(memory_space=VMEM)] * len(fields),
         out_specs=pl.BlockSpec(memory_space=VMEM),
         scratch_shapes=[
@@ -574,6 +585,9 @@
             scratch(dirs, 2),
             scratch(plan.layers),
             pltpu.VMEM((3, plan.layers, plan.grid_rows, LANES), jnp.float32),
+            pltpu.SMEM((plan.layers, 2, dirs), jnp.int32),
+            pltpu.SMEM((plan.layers,), jnp.float32),
+            pltpu.SemaphoreType.DMA((2,)),
         ],
         name="solve",
     )(layer_offsets.transpose(1, 2, 0), reg_weight, *fields)

time: 46.3 us -> 46.2 us (level)
  no operation moved by 1% of the time
where the time goes in v6:
time: 46.2 us; the launch traced here: 46 us
  blocking collectives  22.7 us (49%)
  Pallas kernels  11.6 us (25%)
  waiting for transfers between devices  6.24 us (14%)
  starting transfers between devices  4.73 us (10%)
  between operations  0.67 us (1%)
    all_to_all x1, blocking collectives, per_device(): blocks = lax.all_to_all(blocks, ('layer', 'tile'), 0, 0)  22.7 us
    pallas_call x1, Pallas kernels, per_device(): pl.pallas_call(functools.partial(solve_kernel, plan), out_shape=kind((pla...  6.99 us
    ppermute x3, waiting for transfers between devices, per_device(): lax.ppermute(sent[k], 'tile', [(i, i ^ 2 * k) for i in range(plan.tiles)])  4.89 us
    ppermute x3, starting transfers between devices, per_device(): lax.ppermute(sent[k], 'tile', [(i, i ^ 2 * k) for i in range(plan.tiles)])  4.7 us
    pallas_call x2, Pallas kernels, gather(): pl.pallas_call(functools.partial(gather_kernel, plan, slots), out_shape=[...  3.41 us
    ppermute x4, waiting for transfers between devices, per_device(): fields = fields + [lax.ppermute(field, 'tile', swap) for field in fields]  1.35 us
    pallas_call x1, Pallas kernels, combine(): pl.pallas_call(functools.partial(combine_kernel, plan), out_shape=[jax.Sh...  1.23 us
  transfers between devices with their start and end apart: 7, of which 5 were waited for; matrix products, arithmetic and copies ran while one was open for 0% of the time, Pallas kernels for 4%

profile of v6, /device:TPU:0, one launch (start us, length us, event | category | flops | bytes accessed | tf_op | source)
XLA Modules:
  0.0 46.0 jit_solution(3043091739413451384)
XLA Ops:
  0.6 1.7 %gather.2 = (f32[272,128]{1,0:T(8,128)S(1)}, f32[272,128]{1,0:T(8,128)S(1)}) custom-call(f32[6,12,64,128]{3,2,1,0:T(8,128)} %bitcast.8, s32[12,4096]{1,0:T(8,128)} %mask.3), custom_call_target="tpu_custom_call" | custom-call | flops 10000000 | bytes 2000000 | tf_op jit(solution)/shard_map/gather/pallas_call | solution.py:537
  2.4 0.0 copy-start
  2.4 4.0 %collective-permute-start.2 = (f32[272,128]{1,0:T(8,128)S(1)}, f32[272,128]{1,0:T(8,128)S(1)}, u32[]{:S(2)}, u32[]{:S(2)}) collective-permute-start(f32[272,128]{1,0:T(8,128)S(1)} %get-tuple-element.11), channel_id=1, source_target_pairs={{0,6},{1,7},{2,4},{3,5},{4,2},{5,3},{6,0},{7,1},{8,14},{9,15},{10,... | collective-permute-start | bytes 417800 | tf_op jit(solution)/shard_map/ppermute | solution.py:563
  6.4 0.5 %collective-permute-start.1 = (f32[272,128]{1,0:T(8,128)S(1)}, f32[272,128]{1,0:T(8,128)S(1)}, u32[]{:S(2)}, u32[]{:S(2)}) collective-permute-start(f32[272,128]{1,0:T(8,128)S(1)} %get-tuple-element.8.refs_0_), channel_id=1, source_target_pairs={{0,4},{1,5},{2,6},{3,7},{4,0},{5,1},{6,2},{7,3},{8,12},{9,13},{10,... | collective-permute-start | bytes 417800 | tf_op jit(solution)/shard_map/ppermute | solution.py:563
  6.9 0.0 copy-done
  6.9 1.7 %gather.3 = (f32[272,128]{1,0:T(8,128)S(1)}, f32[272,128]{1,0:T(8,128)S(1)}) custom-call(f32[6,12,64,128]{3,2,1,0:T(8,128)} %bitcast.9, s32[12,4096]{1,0:T(8,128)} %mask.3, f32[272,128]{1,0:T(8,128)} %copy-done), custom_call_target="tpu_custom_call" | custom-call | flops 10000000 | bytes 2000000 | tf_op jit(solution)/shard_map/gather/pallas_call | solution.py:537
  8.6 0.2 collective-permute-start
  8.8 0.0 collective-permute-start.3
  8.8 1.5 %collective-permute-done.2.refs_3_ = f32[272,128]{1,0:T(8,128)S(1)} collective-permute-done((f32[272,128]{1,0:T(8,128)S(1)}, f32[272,128]{1,0:T(8,128)S(1)}, u32[]{:S(2)}, u32[]{:S(2)}) %collective-permute-start.2) | collective-permute-done | bytes 139296 | tf_op jit(solution)/shard_map/ppermute | solution.py:563
  10.2 0.0 collective-permute-start.6
  10.2 2.8 %collective-permute-done.1.refs_2_ = f32[272,128]{1,0:T(8,128)S(1)} collective-permute-done((f32[272,128]{1,0:T(8,128)S(1)}, f32[272,128]{1,0:T(8,128)S(1)}, u32[]{:S(2)}, u32[]{:S(2)}) %collective-permute-start.1) | collective-permute-done | bytes 139296 | tf_op jit(solution)/shard_map/ppermute | solution.py:563
  13.0 0.0 collective-permute-start.5
  13.0 0.7 %collective-permute-done.refs_1_ = f32[272,128]{1,0:T(8,128)S(1)} collective-permute-done((f32[272,128]{1,0:T(8,128)S(1)}, f32[272,128]{1,0:T(8,128)S(1)}, u32[]{:S(2)}, u32[]{:S(2)}) %collective-permute-start) | collective-permute-done | bytes 139296 | tf_op jit(solution)/shard_map/ppermute | solution.py:563
  13.7 0.0 collective-permute-start.4
  13.7 0.0 collective-permute-done.3.refs_4_
  13.7 0.0 collective-permute-done.6.refs_7_
  13.7 0.7 %collective-permute-done.5.refs_6_ = f32[272,128]{1,0:T(8,128)S(1)} collective-permute-done((f32[272,128]{1,0:T(8,128)S(1)}, f32[272,128]{1,0:T(8,128)S(1)}, u32[]{:S(2)}, u32[]{:S(2)}) %collective-permute-start.5) | collective-permute-done | bytes 139296 | tf_op jit(solution)/shard_map/ppermute | solution.py:565
  14.4 0.7 %collective-permute-done.4.refs_5_ = f32[272,128]{1,0:T(8,128)S(1)} collective-permute-done((f32[272,128]{1,0:T(8,128)S(1)}, f32[272,128]{1,0:T(8,128)S(1)}, u32[]{:S(2)}, u32[]{:S(2)}) %collective-permute-start.4) | collective-permute-done | bytes 139296 | tf_op jit(solution)/shard_map/ppermute | solution.py:565
  15.0 7.0 %solve.1 = f32[32,40,128]{2,1,0:T(8,128)S(1)} custom-call(s32[4,2,6]{2,1,0:T(2,128)} %bitcast.10, f32[4]{0:T(128)} %all_weights.1, f32[272,128]{1,0:T(8,128)S(1)} %get-tuple-element.9.refs_0_, f32[272,128]{1,0:T(8,128)S(1)} %collective-permute-done.refs_1_, f32[272,128]{1,0:T(8,128)S(1)} %collective-permute-done.1.refs_2_, ...), custom_call_target="tpu_custom_call" | custom-call | tf_op jit(solution)/shard_map/solve/pallas_call | solution.py:574
  22.0 22.7 %all_to_all.5.blocks = f32[32,40,128]{2,1,0:T(8,128)S(1)} all-to-all(f32[32,40,128]{2,1,0:T(8,128)S(1)} %solve.1), channel_id=1, replica_groups=mesh['layer'=4,'tile'=8] {'layer','tile'}, dimensions={0} | all-to-all | bytes 1310720 | tf_op jit(solution)/shard_map/all_to_all | solution.py:594
  44.8 1.2 %combine.1 = (f32[384,128]{1,0:T(8,128)}, f32[384,128]{1,0:T(8,128)}) custom-call(f32[32,40,128]{2,1,0:T(8,128)S(1)} %all_to_all.5.blocks), custom_call_target="tpu_custom_call" | custom-call | tf_op jit(solution)/shard_map/combine/pallas_call | solution.py:503
Async XLA Ops:
  2.4 4.5 %copy-start = (f32[272,128]{1,0:T(8,128)}, f32[272,128]{1,0:T(8,128)S(1)}, u32[]{:S(2)}) copy-start(f32[272,128]{1,0:T(8,128)S(1)} %get-tuple-element.8.refs_0_) | copy-start | bytes 417796
  2.4 7.9 %collective-permute-start.2 = (f32[272,128]{1,0:T(8,128)S(1)}, f32[272,128]{1,0:T(8,128)S(1)}, u32[]{:S(2)}, u32[]{:S(2)}) collective-permute-start(f32[272,128]{1,0:T(8,128)S(1)} %get-tuple-element.11), channel_id=1, source_target_pairs={{0,6},{1,7},{2,4},{3,5},{4,2},{5,3},{6,0},{7,1},{8,14},{9,15},{10,... | collective-permute-start | bytes 417800 | tf_op jit(solution)/shard_map/ppermute | solution.py:563
  6.4 6.7 %collective-permute-start.1 = (f32[272,128]{1,0:T(8,128)S(1)}, f32[272,128]{1,0:T(8,128)S(1)}, u32[]{:S(2)}, u32[]{:S(2)}) collective-permute-start(f32[272,128]{1,0:T(8,128)S(1)} %get-tuple-element.8.refs_0_), channel_id=1, source_target_pairs={{0,4},{1,5},{2,6},{3,7},{4,0},{5,1},{6,2},{7,3},{8,12},{9,13},{10,... | collective-permute-start | bytes 417800 | tf_op jit(solution)/shard_map/ppermute | solution.py:563
  8.6 5.1 %collective-permute-start = (f32[272,128]{1,0:T(8,128)S(1)}, f32[272,128]{1,0:T(8,128)S(1)}, u32[]{:S(2)}, u32[]{:S(2)}) collective-permute-start(f32[272,128]{1,0:T(8,128)S(1)} %get-tuple-element.10), channel_id=1, source_target_pairs={{0,2},{1,3},{2,0},{3,1},{4,6},{5,7},{6,4},{7,5},{8,10},{9,11},{10,... | collective-permute-start | bytes 417800 | tf_op jit(solution)/shard_map/ppermute | solution.py:563
  8.8 4.9 %collective-permute-start.3 = (f32[272,128]{1,0:T(8,128)S(1)}, f32[272,128]{1,0:T(8,128)S(1)}, u32[]{:S(2)}, u32[]{:S(2)}) collective-permute-start(f32[272,128]{1,0:T(8,128)S(1)} %get-tuple-element.9.refs_0_), channel_id=1, source_target_pairs={{0,1},{1,0},{2,3},{3,2},{4,5},{5,4},{6,7},{7,6},{8,9},{9,8},{10,11... | collective-permute-start | bytes 417800 | tf_op jit(solution)/shard_map/ppermute | solution.py:565
  10.2 3.5 %collective-permute-start.6 = (f32[272,128]{1,0:T(8,128)S(1)}, f32[272,128]{1,0:T(8,128)S(1)}, u32[]{:S(2)}, u32[]{:S(2)}) collective-permute-start(f32[272,128]{1,0:T(8,128)S(1)} %collective-permute-done.2.refs_3_), channel_id=1, source_target_pairs={{0,1},{1,0},{2,3},{3,2},{4,5},{5,4},{6,7},{7,6},{8,9},{9,8},{10,11... | collective-permute-start | bytes 417800 | tf_op jit(solution)/shard_map/ppermute | solution.py:565
  13.0 1.4 %collective-permute-start.5 = (f32[272,128]{1,0:T(8,128)S(1)}, f32[272,128]{1,0:T(8,128)S(1)}, u32[]{:S(2)}, u32[]{:S(2)}) collective-permute-start(f32[272,128]{1,0:T(8,128)S(1)} %collective-permute-done.1.refs_2_), channel_id=1, source_target_pairs={{0,1},{1,0},{2,3},{3,2},{4,5},{5,4},{6,7},{7,6},{8,9},{9,8},{10,11... | collective-permute-start | bytes 417800 | tf_op jit(solution)/shard_map/ppermute | solution.py:565
  13.7 1.4 %collective-permute-start.4 = (f32[272,128]{1,0:T(8,128)S(1)}, f32[272,128]{1,0:T(8,128)S(1)}, u32[]{:S(2)}, u32[]{:S(2)}) collective-permute-start(f32[272,128]{1,0:T(8,128)S(1)} %collective-permute-done.refs_1_), channel_id=1, source_target_pairs={{0,1},{1,0},{2,3},{3,2},{4,5},{5,4},{6,7},{7,6},{8,9},{9,8},{10,11... | collective-permute-start | bytes 417800 | tf_op jit(solution)/shard_map/ppermute | solution.py:565

commit v7 on v6

--- a/solution.py
+++ b/solution.py
@@ -78,15 +78,18 @@
         turn = (-steps) % LANES
     else:
         turn = jnp.where(steps > 0, LANES - steps, -steps)
+    if count == 2:
+        lane = lane_index()
+        other = tall((lane < steps) | (lane >= LANES + steps), rows)
+        return [
+            pltpu.roll(jnp.where(other, tiles[1 - t], tiles[t]), turn, 1) for t in range(2)
+        ]
     turned = [pltpu.roll(tile, turn, 1) for tile in tiles]
     if count == 1:
         return turned
     source = lane_index() + steps
     past = tall(source >= LANES, rows)
     before = tall(source < 0, rows)
-    if count == 2:
-        outside = past | before
-        return [jnp.where(outside, turned[1 - t], turned[t]) for t in range(2)]
     return [
         jnp.where(
             past,
@@ -323,14 +326,16 @@
                 moved = shift(window, -offsets[layer, 1, g])
                 moved = [moved] if level == 2 else moved
                 sums = moved if sums is None else [s + m for s, m in zip(sums, moved)]
-            sums = [0.5 * value for value in sums]
+            if level:
+                sums = [0.5 * value for value in sums]
             if source is not None:
                 weight = weights[layer]
                 sums = [s + weight * value for s, value in zip(sums, laplace(smooth, layer, r, shift))]
             if level == 2:
                 packed[2, layer, r : r + chunk, :] = sums[0]
                 return
-            sums = [s * inside for s, inside in zip(sums, in_grid)]
+            scale = in_grid if level else [0.5 * inside for inside in in_grid]
+            sums = [s * inside for s, inside in zip(sums, scale)]
             for t in tiles:
                 (v0, v1)[level][layer, t, rows_at(r), :] = sums[t]
             packed[level, layer, r : r + chunk, :] = pack(sums)

time: 46.2 us -> 46.2 us (level)
  no operation moved by 1% of the time
where the time goes in v7:
time: 46.2 us; the launch traced here: 46 us
  blocking collectives  22.7 us (49%)
  Pallas kernels  11.6 us (25%)
  waiting for transfers between devices  6.24 us (14%)
  starting transfers between devices  4.73 us (10%)
  between operations  0.67 us (1%)
    all_to_all x1, blocking collectives, per_device(): blocks = lax.all_to_all(blocks, ('layer', 'tile'), 0, 0)  22.7 us
    pallas_call x1, Pallas kernels, per_device(): pl.pallas_call(functools.partial(solve_kernel, plan), out_shape=kind((pla...  6.97 us
    ppermute x3, waiting for transfers between devices, per_device(): lax.ppermute(sent[k], 'tile', [(i, i ^ 2 * k) for i in range(plan.tiles)])  4.89 us
    ppermute x3, starting transfers between devices, per_device(): lax.ppermute(sent[k], 'tile', [(i, i ^ 2 * k) for i in range(plan.tiles)])  4.7 us
    pallas_call x2, Pallas kernels, gather(): pl.pallas_call(functools.partial(gather_kernel, plan, slots), out_shape=[...  3.41 us
    ppermute x4, waiting for transfers between devices, per_device(): fields = fields + [lax.ppermute(field, 'tile', swap) for field in fields]  1.35 us
    pallas_call x1, Pallas kernels, combine(): pl.pallas_call(functools.partial(combine_kernel, plan), out_shape=[jax.Sh...  1.23 us
  transfers between devices with their start and end apart: 7, of which 5 were waited for; matrix products, arithmetic and copies ran while one was open for 0% of the time, Pallas kernels for 4%

profile of v7, /device:TPU:0, one launch (start us, length us, event | category | flops | bytes accessed | tf_op | source)
XLA Modules:
  0.0 46.0 jit_solution(17489423421032476415)
XLA Ops:
  0.6 1.7 %gather.2 = (f32[272,128]{1,0:T(8,128)S(1)}, f32[272,128]{1,0:T(8,128)S(1)}) custom-call(f32[6,12,64,128]{3,2,1,0:T(8,128)} %bitcast.8, s32[12,4096]{1,0:T(8,128)} %mask.3), custom_call_target="tpu_custom_call" | custom-call | flops 10000000 | bytes 2000000 | tf_op jit(solution)/shard_map/gather/pallas_call | solution.py:542
  2.4 0.0 copy-start
  2.4 4.0 %collective-permute-start.2 = (f32[272,128]{1,0:T(8,128)S(1)}, f32[272,128]{1,0:T(8,128)S(1)}, u32[]{:S(2)}, u32[]{:S(2)}) collective-permute-start(f32[272,128]{1,0:T(8,128)S(1)} %get-tuple-element.11), channel_id=1, source_target_pairs={{0,6},{1,7},{2,4},{3,5},{4,2},{5,3},{6,0},{7,1},{8,14},{9,15},{10,... | collective-permute-start | bytes 417800 | tf_op jit(solution)/shard_map/ppermute | solution.py:568
  6.4 0.5 %collective-permute-start.1 = (f32[272,128]{1,0:T(8,128)S(1)}, f32[272,128]{1,0:T(8,128)S(1)}, u32[]{:S(2)}, u32[]{:S(2)}) collective-permute-start(f32[272,128]{1,0:T(8,128)S(1)} %get-tuple-element.8.refs_0_), channel_id=1, source_target_pairs={{0,4},{1,5},{2,6},{3,7},{4,0},{5,1},{6,2},{7,3},{8,12},{9,13},{10,... | collective-permute-start | bytes 417800 | tf_op jit(solution)/shard_map/ppermute | solution.py:568
  6.9 0.0 copy-done
  6.9 1.7 %gather.3 = (f32[272,128]{1,0:T(8,128)S(1)}, f32[272,128]{1,0:T(8,128)S(1)}) custom-call(f32[6,12,64,128]{3,2,1,0:T(8,128)} %bitcast.9, s32[12,4096]{1,0:T(8,128)} %mask.3, f32[272,128]{1,0:T(8,128)} %copy-done), custom_call_target="tpu_custom_call" | custom-call | flops 10000000 | bytes 2000000 | tf_op jit(solution)/shard_map/gather/pallas_call | solution.py:542
  8.6 0.2 collective-permute-start
  8.8 0.0 collective-permute-start.3
  8.8 1.5 %collective-permute-done.2.refs_3_ = f32[272,128]{1,0:T(8,128)S(1)} collective-permute-done((f32[272,128]{1,0:T(8,128)S(1)}, f32[272,128]{1,0:T(8,128)S(1)}, u32[]{:S(2)}, u32[]{:S(2)}) %collective-permute-start.2) | collective-permute-done | bytes 139296 | tf_op jit(solution)/shard_map/ppermute | solution.py:568
  10.2 0.0 collective-permute-start.6
  10.2 2.8 %collective-permute-done.1.refs_2_ = f32[272,128]{1,0:T(8,128)S(1)} collective-permute-done((f32[272,128]{1,0:T(8,128)S(1)}, f32[272,128]{1,0:T(8,128)S(1)}, u32[]{:S(2)}, u32[]{:S(2)}) %collective-permute-start.1) | collective-permute-done | bytes 139296 | tf_op jit(solution)/shard_map/ppermute | solution.py:568
  13.0 0.0 collective-permute-start.5
  13.0 0.7 %collective-permute-done.refs_1_ = f32[272,128]{1,0:T(8,128)S(1)} collective-permute-done((f32[272,128]{1,0:T(8,128)S(1)}, f32[272,128]{1,0:T(8,128)S(1)}, u32[]{:S(2)}, u32[]{:S(2)}) %collective-permute-start) | collective-permute-done | bytes 139296 | tf_op jit(solution)/shard_map/ppermute | solution.py:568
  13.7 0.0 collective-permute-start.4
  13.7 0.0 collective-permute-done.3.refs_4_
  13.7 0.0 collective-permute-done.6.refs_7_
  13.7 0.7 %collective-permute-done.5.refs_6_ = f32[272,128]{1,0:T(8,128)S(1)} collective-permute-done((f32[272,128]{1,0:T(8,128)S(1)}, f32[272,128]{1,0:T(8,128)S(1)}, u32[]{:S(2)}, u32[]{:S(2)}) %collective-permute-start.5) | collective-permute-done | bytes 139296 | tf_op jit(solution)/shard_map/ppermute | solution.py:570
  14.4 0.7 %collective-permute-done.4.refs_5_ = f32[272,128]{1,0:T(8,128)S(1)} collective-permute-done((f32[272,128]{1,0:T(8,128)S(1)}, f32[272,128]{1,0:T(8,128)S(1)}, u32[]{:S(2)}, u32[]{:S(2)}) %collective-permute-start.4) | collective-permute-done | bytes 139296 | tf_op jit(solution)/shard_map/ppermute | solution.py:570
  15.0 7.0 %solve.1 = f32[32,40,128]{2,1,0:T(8,128)S(1)} custom-call(s32[4,2,6]{2,1,0:T(2,128)} %bitcast.10, f32[4]{0:T(128)} %all_weights.1, f32[272,128]{1,0:T(8,128)S(1)} %get-tuple-element.9.refs_0_, f32[272,128]{1,0:T(8,128)S(1)} %collective-permute-done.refs_1_, f32[272,128]{1,0:T(8,128)S(1)} %collective-permute-done.1.refs_2_, ...), custom_call_target="tpu_custom_call" | custom-call | tf_op jit(solution)/shard_map/solve/pallas_call | solution.py:579
  22.0 22.7 %all_to_all.5.blocks = f32[32,40,128]{2,1,0:T(8,128)S(1)} all-to-all(f32[32,40,128]{2,1,0:T(8,128)S(1)} %solve.1), channel_id=1, replica_groups=mesh['layer'=4,'tile'=8] {'layer','tile'}, dimensions={0} | all-to-all | bytes 1310720 | tf_op jit(solution)/shard_map/all_to_all | solution.py:599
  44.7 1.2 %combine.1 = (f32[384,128]{1,0:T(8,128)}, f32[384,128]{1,0:T(8,128)}) custom-call(f32[32,40,128]{2,1,0:T(8,128)S(1)} %all_to_all.5.blocks), custom_call_target="tpu_custom_call" | custom-call | tf_op jit(solution)/shard_map/combine/pallas_call | solution.py:508
Async XLA Ops:
  2.4 4.5 %copy-start = (f32[272,128]{1,0:T(8,128)}, f32[272,128]{1,0:T(8,128)S(1)}, u32[]{:S(2)}) copy-start(f32[272,128]{1,0:T(8,128)S(1)} %get-tuple-element.8.refs_0_) | copy-start | bytes 417796
  2.4 7.9 %collective-permute-start.2 = (f32[272,128]{1,0:T(8,128)S(1)}, f32[272,128]{1,0:T(8,128)S(1)}, u32[]{:S(2)}, u32[]{:S(2)}) collective-permute-start(f32[272,128]{1,0:T(8,128)S(1)} %get-tuple-element.11), channel_id=1, source_target_pairs={{0,6},{1,7},{2,4},{3,5},{4,2},{5,3},{6,0},{7,1},{8,14},{9,15},{10,... | collective-permute-start | bytes 417800 | tf_op jit(solution)/shard_map/ppermute | solution.py:568
  6.4 6.7 %collective-permute-start.1 = (f32[272,128]{1,0:T(8,128)S(1)}, f32[272,128]{1,0:T(8,128)S(1)}, u32[]{:S(2)}, u32[]{:S(2)}) collective-permute-start(f32[272,128]{1,0:T(8,128)S(1)} %get-tuple-element.8.refs_0_), channel_id=1, source_target_pairs={{0,4},{1,5},{2,6},{3,7},{4,0},{5,1},{6,2},{7,3},{8,12},{9,13},{10,... | collective-permute-start | bytes 417800 | tf_op jit(solution)/shard_map/ppermute | solution.py:568
  8.6 5.1 %collective-permute-start = (f32[272,128]{1,0:T(8,128)S(1)}, f32[272,128]{1,0:T(8,128)S(1)}, u32[]{:S(2)}, u32[]{:S(2)}) collective-permute-start(f32[272,128]{1,0:T(8,128)S(1)} %get-tuple-element.10), channel_id=1, source_target_pairs={{0,2},{1,3},{2,0},{3,1},{4,6},{5,7},{6,4},{7,5},{8,10},{9,11},{10,... | collective-permute-start | bytes 417800 | tf_op jit(solution)/shard_map/ppermute | solution.py:568
  8.8 4.9 %collective-permute-start.3 = (f32[272,128]{1,0:T(8,128)S(1)}, f32[272,128]{1,0:T(8,128)S(1)}, u32[]{:S(2)}, u32[]{:S(2)}) collective-permute-start(f32[272,128]{1,0:T(8,128)S(1)} %get-tuple-element.9.refs_0_), channel_id=1, source_target_pairs={{0,1},{1,0},{2,3},{3,2},{4,5},{5,4},{6,7},{7,6},{8,9},{9,8},{10,11... | collective-permute-start | bytes 417800 | tf_op jit(solution)/shard_map/ppermute | solution.py:570
  10.2 3.5 %collective-permute-start.6 = (f32[272,128]{1,0:T(8,128)S(1)}, f32[272,128]{1,0:T(8,128)S(1)}, u32[]{:S(2)}, u32[]{:S(2)}) collective-permute-start(f32[272,128]{1,0:T(8,128)S(1)} %collective-permute-done.2.refs_3_), channel_id=1, source_target_pairs={{0,1},{1,0},{2,3},{3,2},{4,5},{5,4},{6,7},{7,6},{8,9},{9,8},{10,11... | collective-permute-start | bytes 417800 | tf_op jit(solution)/shard_map/ppermute | solution.py:570
  13.0 1.4 %collective-permute-start.5 = (f32[272,128]{1,0:T(8,128)S(1)}, f32[272,128]{1,0:T(8,128)S(1)}, u32[]{:S(2)}, u32[]{:S(2)}) collective-permute-start(f32[272,128]{1,0:T(8,128)S(1)} %collective-permute-done.1.refs_2_), channel_id=1, source_target_pairs={{0,1},{1,0},{2,3},{3,2},{4,5},{5,4},{6,7},{7,6},{8,9},{9,8},{10,11... | collective-permute-start | bytes 417800 | tf_op jit(solution)/shard_map/ppermute | solution.py:570
  13.7 1.4 %collective-permute-start.4 = (f32[272,128]{1,0:T(8,128)S(1)}, f32[272,128]{1,0:T(8,128)S(1)}, u32[]{:S(2)}, u32[]{:S(2)}) collective-permute-start(f32[272,128]{1,0:T(8,128)S(1)} %collective-permute-done.refs_1_), channel_id=1, source_target_pairs={{0,1},{1,0},{2,3},{3,2},{4,5},{5,4},{6,7},{7,6},{8,9},{9,8},{10,11... | collective-permute-start | bytes 417800 | tf_op jit(solution)/shard_map/ppermute | solution.py:570
